TPU v7x, 256 devices: a whole 4x4x8 slice. The times are simulated.
256 devices in a mesh: row: 32 (over x_lo, z, core), col: 8 (over y, x_hi).
Axes of the slice: x: 4 (x_hi: 2, x_lo: 2; x = x_hi * 2 + x_lo), y: 4, z: 8, core: 2. Of those that a mesh axis runs over, the one named last changes fastest.
Arguments:
- hessian: float32 [14336, 14336], P('row', 'col'), may hold values from -1 to 6, as said below
- dense_weight: float32 [14336, 1024], P('col', 'row'), may hold values from -6 to 6
- start_iterate: float32 [14336, 1024], P('col', 'row'), may hold values from -6 to 6
- start_multiplier: float32 [14336, 1024], P('col', 'row'), may hold values from -3 to 3
- keep_mask: int32 [14336, 1024], P('col', 'row'), may hold values 0 or 1
Outputs:
- iterate: float32 [14336, 1024], P('col', 'row')
- projected: float32 [14336, 1024], P('col', 'row')
- multiplier: float32 [14336, 1024], P('col', 'row')
Inputs may be any that keep to these rules, and one draw needn't show every extreme that they name: `hessian`: a calibration Hessian: symmetric up to rounding and positive definite.
All inputs are finite; a program needn't handle non-finite values. No bound on the sum of `keep_mask` on one device may be relied on, other than what follows from the above.
Results may differ from a plain program's by a relative error of at most 0.0001.
Values sent between devices are 32-bit elements; how exact they have to be, the bound alone decides.
A program may use at most 64 MiB of HBM per device.

v0:
```python
import jax
import jax.numpy as jnp
from jax import lax
from jax.sharding import PartitionSpec as P

ITERS = 2


step_size = 0.25
penalty = 1.0


def split_up(array, dim, length):
    before, after = (array.shape[:dim], array.shape[dim + 1 :])
    return jnp.moveaxis(array.reshape(*before, length, -1, *after), dim, 0)


def sum_at_owner(array, axis, dim):
    tiles = split_up(array, dim, lax.axis_size(axis))
    arrived = lax.all_to_all(tiles, axis, split_axis=0, concat_axis=0, tiled=True)
    return arrived.sum(axis=0)


def per_device(hessian, dense_weight, start_iterate, start_multiplier, keep_mask):
    keeping = keep_mask.astype(jnp.float32)
    iterate = start_iterate
    multiplier = start_multiplier
    projected = keeping * (iterate + multiplier)
    for rounds in range(ITERS):
        change = iterate - dense_weight
        gathered = lax.all_gather(change, "row", axis=1, tiled=True)
        partial_value = jnp.dot(
            hessian, gathered, precision=lax.Precision.HIGHEST, preferred_element_type=jnp.float32
        )
        summed = sum_at_owner(partial_value, "col", 0)
        shaped = summed.reshape(1, 1, summed.shape[0], summed.shape[1])
        relaid = lax.all_to_all(
            lax.all_to_all(shaped, "row", split_axis=3, concat_axis=0, tiled=True),
            "col",
            split_axis=0,
            concat_axis=1,
            tiled=True,
        )
        gradient = relaid.reshape(iterate.shape)
        iterate = iterate - step_size * (gradient + penalty * (iterate - projected + multiplier))
        projected = keeping * (iterate + multiplier)
        multiplier = multiplier + iterate - projected
    return (iterate, projected, multiplier)


def solution(mesh):
    return jax.shard_map(
        per_device,
        mesh=mesh,
        in_specs=(
            P("row", "col"),
            P("col", "row"),
            P("col", "row"),
            P("col", "row"),
            P("col", "row"),
        ),
        out_specs=(P("col", "row"), P("col", "row"), P("col", "row")),
        check_vma=False,
    )
```

profile of v0, /device:TPU:8, one launch (start us, length us, event | category | flops | bytes accessed | tf_op | source)
XLA Modules:
  0.0 362.9 jit_solution(16763132833857299460)
XLA Ops:
  7.2 0.0 copy-start
  7.2 0.0 all-gather.3.cloned.1.call-start
  7.2 1.9 sub.24
  9.1 0.0 all-gather.3.cloned.1.call-update
  9.2 0.0 all-gather.5.cloned.1.call-start
  9.2 75.0 %all-gather.3.cloned.1.call-done = f32[1792,1024]{0,1:T(8,128)} async-done(((f32[1792,32]{0,1:T(8,128)}), f32[1792,1024]{0,1:T(8,128)}) %all-gather.3.cloned.1.call-update) | async-done | bytes 7340048 | tf_op jit(solution)/shard_map/all_gather | solution.py:31
  84.2 0.0 copy-done
  84.2 12.9 %fusion.4 = f32[1024,448]{0,1:T(8,128)S(1)} fusion(f32[1792,1024]{0,1:T(8,128)} %all-gather.3.cloned.1.call-done, f32[448,1792]{1,0:T(8,128)S(1)} %copy-done), kind=kOutput, calls=%fused_computation.8 | convolution fusion | flops 9865003008 | bytes 12386304 | tf_op jit(solution)/shard_map/dot_general | solution.py:32
  97.2 31.4 %all_to_all.76 = f32[8,56,1024]{2,1,0:T(8,128)} all-to-all(f32[8,56,1024]{2,1,0:T(8,128)S(1)} %bitcast.54), channel_id=1, replica_groups=mesh['row'=32,'col'=8] {'col'}, dimensions={0} | all-to-all | bytes 3670016 | tf_op jit(solution)/shard_map/all_to_all | solution.py:20
  128.6 1.6 reduce_sum.18
  130.2 1.0 copy.10
  131.2 0.5 broadcast.8
  131.7 3.8 %reduce = f32[1024,56]{1,0:T(8,128)} reduce(f32[1024,1,1,56]{3,2,1,0:T(1,128)} %bitcast.48, f32[]{:T(128)} %broadcast.8), dimensions={1,2}, to_apply=%bitcast.36.reduce_sub_computation | reduce | bytes 458756
  135.5 0.0 copy-start.1
  135.5 2.3 reshape.32
  137.8 18.5 %all_to_all.77 = f32[32,1,1792]{2,1,0:T(1,128)} all-to-all(f32[32,1,1792]{2,1,0:T(1,128)} %reshape.32), channel_id=1, replica_groups=mesh['row'=32,'col'=8] {'row'}, dimensions={0} | all-to-all | bytes 458752 | tf_op jit(solution)/shard_map/all_to_all | solution.py:38
  156.3 2.8 reduce.1
  159.1 2.8 reshape.33
  161.9 2.3 reshape.34
  164.2 12.6 %all_to_all.78 = f32[8,1,7168]{2,1,0:T(1,128)} all-to-all(f32[8,1,7168]{2,1,0:T(1,128)} %reshape.34), channel_id=1, replica_groups=mesh['row'=32,'col'=8] {'col'}, dimensions={0} | all-to-all | bytes 458752 | tf_op jit(solution)/shard_map/all_to_all | solution.py:37
  176.8 2.8 reduce.2
  179.6 2.2 reshape.35
  181.8 2.2 copy.12
  183.9 2.0 reshape.28
  186.0 0.0 copy-done.1
  186.0 2.1 fusion.3
  188.1 0.0 all-gather.5.cloned.1.call-update
  188.1 64.6 %all-gather.5.cloned.1.call-done = f32[1792,1024]{0,1:T(8,128)} async-done(((f32[1792,32]{0,1:T(8,128)}), f32[1792,1024]{0,1:T(8,128)}) %all-gather.5.cloned.1.call-update) | async-done | bytes 7340048 | tf_op jit(solution)/shard_map/all_gather | solution.py:31
  252.7 12.9 %fusion.5 = f32[1024,448]{0,1:T(8,128)S(1)} fusion(f32[1792,1024]{0,1:T(8,128)} %all-gather.5.cloned.1.call-done, f32[448,1792]{1,0:T(8,128)S(1)} %copy-done), kind=kOutput, calls=%fused_computation.9 | convolution fusion | flops 9865003008 | bytes 12386304 | tf_op jit(solution)/shard_map/dot_general | solution.py:32
  265.7 31.4 %all_to_all.79 = f32[8,56,1024]{2,1,0:T(8,128)} all-to-all(f32[8,56,1024]{2,1,0:T(8,128)S(1)} %bitcast.55), channel_id=1, replica_groups=mesh['row'=32,'col'=8] {'col'}, dimensions={0} | all-to-all | bytes 3670016 | tf_op jit(solution)/shard_map/all_to_all | solution.py:20
  297.1 1.6 reduce_sum.19
  298.7 1.0 copy.13
  299.7 3.8 %reduce.3 = f32[1024,56]{1,0:T(8,128)} reduce(f32[1024,1,1,56]{3,2,1,0:T(1,128)} %bitcast.51, f32[]{:T(128)} %broadcast.8), dimensions={1,2}, to_apply=%bitcast.40.reduce_sub_computation | reduce | bytes 458756
  303.5 0.0 copy-start.2
  303.5 2.3 reshape.36
  305.8 18.5 %all_to_all.80 = f32[32,1,1792]{2,1,0:T(1,128)} all-to-all(f32[32,1,1792]{2,1,0:T(1,128)} %reshape.36), channel_id=1, replica_groups=mesh['row'=32,'col'=8] {'row'}, dimensions={0} | all-to-all | bytes 458752 | tf_op jit(solution)/shard_map/all_to_all | solution.py:38
  324.3 2.8 reduce.4
  327.1 2.8 reshape.37
  329.9 2.3 reshape.38
  332.2 12.6 %all_to_all.81 = f32[8,1,7168]{2,1,0:T(1,128)} all-to-all(f32[8,1,7168]{2,1,0:T(1,128)} %reshape.38), channel_id=1, replica_groups=mesh['row'=32,'col'=8] {'col'}, dimensions={0} | all-to-all | bytes 458752 | tf_op jit(solution)/shard_map/all_to_all | solution.py:37
  344.8 2.8 reduce.5
  347.6 2.2 reshape.39
  349.8 2.2 copy.15
  351.9 2.0 reshape.31
  353.9 0.0 copy-done.2
  353.9 2.1 fusion.2
Async XLA Ops:
  7.2 77.1 %copy-start = (f32[448,1792]{1,0:T(8,128)S(1)}, f32[448,1792]{1,0:T(8,128)}, u32[]{:S(2)}) copy-start(f32[448,1792]{1,0:T(8,128)} %param.5) | copy-start | bytes 9633796
  7.2 77.1 %all-gather.3.cloned.1.call-start = ((), (), s32[]{:S(2)}) async-start(), calls=%async_computation.6 | async-start | bytes 7569408 | tf_op jit(solution)/shard_map/all_gather | solution.py:31
  9.2 243.6 %all-gather.5.cloned.1.call-start = ((), (), s32[]{:S(2)}) async-start(), calls=%async_computation.7 | async-start | bytes 7569408 | tf_op jit(solution)/shard_map/all_gather | solution.py:31
  135.5 50.5 %copy-start.1 = (s32[1792,32]{0,1:T(8,128)S(1)}, s32[1792,32]{0,1:T(8,128)}, u32[]{:S(2)}) copy-start(s32[1792,32]{0,1:T(8,128)} %param.9) | copy-start | bytes 688132
  303.5 50.4 %copy-start.2 = (s32[1792,32]{0,1:T(8,128)S(1)}, s32[1792,32]{0,1:T(8,128)}, u32[]{:S(2)}) copy-start(s32[1792,32]{0,1:T(8,128)} %param.9) | copy-start | bytes 688132
Sparse Core Ops, SparseCore 0:
  10.4 73.7 all-gather.2
  188.2 64.4 all-gather.4
where the time goes:
time: 364 us; the launch traced here: 363 us
  waiting for transfers between devices  140 us (38%)
  blocking collectives  125 us (34%)
  local copies, waits for them, and re-layouts  29.9 us (8%)
  other arithmetic  28.2 us (8%)
  matrix products  25.8 us (7%)
  between operations  14.1 us (4%)
    all_gather x2, waiting for transfers between devices, per_device(): gathered = lax.all_gather(change, 'row', axis=1, tiled=True)  140 us
    all_to_all x2, blocking collectives, sum_at_owner(): lax.all_to_all(tiles, axis, split_axis=0, concat_axis=0, tiled=True)  62.8 us
    all_to_all x2, blocking collectives, per_device(): lax.all_to_all(shaped, 'row', split_axis=3, concat_axis=0, tiled=True)  37 us
    dot_general x2, matrix products, per_device(): jnp.dot(hessian, gathered, precision=lax.Precision.HIGHEST, preferred_ele...  25.8 us
    all_to_all x2, blocking collectives, per_device(): lax.all_to_all(lax.all_to_all(shaped, 'row', split_axis=3, concat_axis=0,...  25.2 us
    unnamed x15, local copies, waits for them, and re-layouts  19.6 us
    unnamed x2, other arithmetic  7.59 us
  transfers between devices with their start and end apart: 2, of which 2 were waited for; matrix products, arithmetic and copies ran while one was open for 0% of the time, Pallas kernels for 0%

commit v1 on v0

v1 whole, which is shorter than its diff:
```python
import jax
import jax.numpy as jnp
from jax import lax
from jax.experimental import pallas as pl
from jax.experimental.pallas import tpu as pltpu
from jax.sharding import PartitionSpec as P

MESH = pl.DeviceIdType.MESH
STEP = 0.25
U = 4
KC = 1792
KR = 896
F32 = jnp.float32
BF16 = jnp.bfloat16


def make_schedule():
    items = []
    gap, hop = 6.4, 2.0
    for u in range(U):
        t = u * gap
        for s in range(6):
            items.append((t + s * hop, u, "ag", s))
        t += 5 * hop + 0.1
        items.append((t, u, "mm", 0))
        t += 5.0
        items.append((t, u, "rsy2", 0))
        t += 3.5
        items.append((t, u, "xhi", 0))
        t += 4.5
        items.append((t, u, "agy1", 0))
        t += 3.5
        items.append((t, u, "agy2", 0))
        t += 4.0
        items.append((t, u, "mmt", 0))
        t += 2.5
        for s in range(1, 6):
            items.append((t + s * hop, u, "rs", s))
    return sorted(items)


SCHEDULE = make_schedule()


def kernel(
    h_ref, c0_ref, a_ref, c1_out, g1_out,
    hbuf, hhi, hlo, xs_ref, xall, pbuf, rb1, rb2, vbuf, xb, c1all, cs_ref, qbuf,
    rx1, rza, rzb, rpa, rpb, rxf, ab, ch, ss, rs, hs,
):
    row = lax.axis_index("row")
    col = lax.axis_index("col")
    k = row % 2
    z = (row // 2) % 8
    x = row // 16
    y = col // 2
    xh = col % 2
    d = 1 - 2 * k
    xo = 1 - x

    def zi(off):
        return (z + d * off + 16) % 8

    def dev_z(off):
        return (x * 16 + zi(off) * 2 + k, col)

    dev_a, dev_b = dev_z(1), dev_z(-1)
    dev_x = (xo * 16 + z * 2 + k, col)
    dev_core = (x * 16 + z * 2 + (1 - k), col)
    y1 = y + 1 - 2 * (y % 2)
    y3 = 3 - y
    dev_y1 = (row, y1 * 2 + xh)
    dev_y3 = (row, y3 * 2 + xh)
    dev_xh = (row, y * 2 + (1 - xh))

    b0, b1 = y % 2, y // 2
    bx = (b0 + b1) % 2
    f1 = (bx, b1)
    f2 = (1 - b1, 1 - b0)
    q = (2 * f1[0] + f2[0], 2 * f1[1] + f2[1])

    cblk = y * 2 + xh
    qz = z // 2
    e0, e1 = qz % 2, qz // 2
    ya_b1 = 1 - e0
    ya_b0 = (e1 + ya_b1) % 2
    y_if0 = 2 * ya_b1 + ya_b0
    y_if1 = 2 * e1 + (1 - e0)
    yd = (1 - x) * y_if0 + x * y_if1
    dev_out = []
    for h in range(2):
        r = 2 * cblk + h
        dev_out.append(((r // 8) * 16 + (r % 8) * 2 + k, yd * 2 + x))
    rblk = x * 8 + z
    qh = (1 - xh) * q[0] + xh * q[1]
    dev_in = [(xh * 16 + (2 * qh + i) * 2 + k, rblk // 2) for i in range(2)]
    hpart = rblk % 2

    barrier = pltpu.get_barrier_semaphore()
    peers = [dev_a, dev_b, dev_x, dev_core, dev_y1, dev_y3, dev_xh] + dev_out + dev_in
    for p in peers:
        pl.semaphore_signal(barrier, inc=1, device_id=p, device_id_type=MESH)
    pl.semaphore_wait(barrier, len(peers))

    names = {}
    sends = []

    def sem(name):
        return names.setdefault(name, len(names))

    def send(name, src, dst, dev):
        i = sem(name)
        c = pltpu.make_async_remote_copy(
            src_ref=src, dst_ref=dst, send_sem=ss.at[i], recv_sem=rs.at[i],
            device_id=dev, device_id_type=MESH,
        )
        c.start()
        sends.append(c)

    def wait(name, slot):
        i = sem(name)
        pltpu.make_async_remote_copy(
            src_ref=slot, dst_ref=slot, send_sem=ss.at[i], recv_sem=rs.at[i],
            device_id=dev_x, device_id_type=MESH,
        ).wait_recv()

    LO = pl.ds(0, KR)
    HI = pl.ds(KR, KR)

    hcopy = pltpu.make_async_copy(h_ref, hbuf.at[k], hs.at[0])

    def start_h():
        hcopy.start()
        send("h", h_ref, hbuf.at[k], dev_core)

    def split_rows(part):
        @pl.loop(0, 28)
        def _(i):
            r0 = pl.multiple_of(i * 16, 16)
            v = hbuf[part, pl.ds(r0, 16), :]
            hi = v.astype(BF16)
            o0 = pl.multiple_of(part * 448 + i * 16, 16)
            hhi[pl.ds(o0, 16), :] = hi
            hlo[pl.ds(o0, 16), :] = (v - hi.astype(F32)).astype(BF16)

    def ag(u, s):
        full = lambda o: xall.at[u, x, zi(o)]
        if s == 0:
            xall[u, x, z] = c0_ref[u]
            send(f"fa{u}.1", c0_ref.at[u], full(0), dev_a)
            send(f"fb{u}.1", c0_ref.at[u], full(0), dev_b)
            send(f"x{u}", c0_ref.at[u], full(0), dev_x)
            return
        par = lambda o: xall.at[u, xo, zi(o), :, HI]
        low = lambda o: xall.at[u, x, zi(o), :, LO]
        if s <= 4:
            wait(f"fa{u}.{s}", full(-s))
            if s < 4:
                send(f"fa{u}.{s + 1}", full(-s), full(-s), dev_a)
        if s <= 3:
            wait(f"fb{u}.{s}", full(s))
            if s < 3:
                send(f"fb{u}.{s + 1}", full(s), full(s), dev_b)
        if s == 1:
            wait(f"x{u}", xall.at[u, xo, z])
            send(f"pa{u}.1", par(0), par(0), dev_a)
            send(f"pb{u}.1", par(0), par(0), dev_b)
        elif s <= 5:
            if s - 1 <= 3:
                wait(f"pa{u}.{s - 1}", par(-(s - 1)))
                if s - 1 < 3:
                    send(f"pa{u}.{s}", par(-(s - 1)), par(-(s - 1)), dev_a)
            wait(f"pb{u}.{s - 1}", par(s - 1))
            if s - 1 < 4:
                send(f"pb{u}.{s}", par(s - 1), par(s - 1), dev_b)
        if s <= 4:
            send(f"xa{u}.{s}", low(-s), low(-s), dev_x)
        if s <= 3:
            send(f"xb{u}.{s}", low(s), low(s), dev_x)
        if s == 5:
            olow = lambda o: xall.at[u, xo, zi(o), :, LO]
            for j in range(1, 5):
                wait(f"xa{u}.{j}", olow(-j))
            for j in range(1, 4):
                wait(f"xb{u}.{j}", olow(j))

    NT = (((1,), (1,)), ((), ()))
    NN = (((1,), (0,)), ((), ()))

    def mm(u):
        for half in range(2):
            split_half(xall, u, half, xs_ref, KC)
        lhs = xs_ref[...]

        def part(c0, n):
            r = lax.dot_general(lhs, hhi[pl.ds(c0, n), :], NT, preferred_element_type=F32)
            r2 = lax.dot_general(lhs[:128], hlo[pl.ds(c0, n), :], NT, preferred_element_type=F32)
            v = (r[:128] + r[128:] + r2) * (-STEP)
            return v.reshape(2, 8, 8, n)

        @pl.loop(0, 3)
        def _(j):
            c0 = pl.multiple_of(j * 256, 256)
            pbuf[u, :, :, :, pl.ds(c0, 256)] = part(c0, 256)

        pbuf[u, :, :, :, pl.ds(768, 128)] = part(768, 128)
        send(f"r1{u}.0", pbuf.at[u, 0, pl.ds(4 * (1 - f1[0]), 4)], rb1.at[u, 0], dev_y1)
        send(f"r1{u}.1", pbuf.at[u, 1, pl.ds(4 * (1 - f1[1]), 4)], rb1.at[u, 1], dev_y3)

    def split_half(src, u, half, dst, width):
        @pl.loop(0, 4)
        def _(i):
            v = src[u, half, pl.ds(i * 2, 2)].reshape(16, width)
            hi = v.astype(BF16)
            r0 = half * 64 + i * 16
            dst[pl.ds(pl.multiple_of(r0, 16), 16), :] = hi
            dst[pl.ds(pl.multiple_of(128 + r0, 16), 16), :] = (v - hi.astype(F32)).astype(BF16)

    def rsy2(u):
        for hf, dev2 in ((0, dev_y3), (1, dev_y1)):
            wait(f"r1{u}.{hf}", rb1.at[u, hf])
            base = 4 * f1[hf]
            o = 2 * (1 - f2[hf])
            pbuf[u, hf, pl.ds(base + o, 2)] = pbuf[u, hf, pl.ds(base + o, 2)] + rb1[u, hf, pl.ds(o, 2)]
            send(f"r2{u}.{hf}", pbuf.at[u, hf, pl.ds(base + o, 2)], rb2.at[u, hf], dev2)
        for hf in range(2):
            o = 2 * f2[hf]
            vbuf[u, hf] = pbuf[u, hf, pl.ds(4 * f1[hf] + o, 2)] + rb1[u, hf, pl.ds(o, 2)]
        for i in range(2):
            wait_a(u, i)
        vbuf[u, xh] = vbuf[u, xh] + ab[u]

    def wait_a(u, i):
        n0 = sem(f"a{u}.{i}")
        pltpu.make_async_remote_copy(
            src_ref=ab.at[u, i], dst_ref=ab.at[u, i], send_sem=ss.at[n0], recv_sem=rs.at[n0],
            device_id=dev_x, device_id_type=MESH,
        ).wait_recv()

    def xhi(u):
        for hf in range(2):
            wait(f"r2{u}.{hf}", rb2.at[u, hf])
            vbuf[u, hf] = vbuf[u, hf] + rb2[u, hf]
        send(f"xh{u}", vbuf.at[u], xb.at[u], dev_xh)

    def agy1(u):
        wait(f"xh{u}", xb.at[u])
        for hf, dev in ((0, dev_y3), (1, dev_y1)):
            slot = c1all.at[u, hf, pl.ds(2 * q[hf], 2)]
            c1all[u, hf, pl.ds(2 * q[hf], 2)] = vbuf[u, hf] + xb[u, hf]
            send(f"g1{u}.{hf}", slot, slot, dev)
        for i in range(2):
            send_home(u, i)

    def send_home(u, i):
        src = c1all.at[u, xh, 2 * qh + i]
        n0 = sem(f"c{u}.{i}")
        c = pltpu.make_async_remote_copy(
            src_ref=src, dst_ref=ch.at[u, hpart], send_sem=ss.at[n0],
            recv_sem=rs.at[sem(f"c{u}.0r") + hpart],
            device_id=dev_in[i], device_id_type=MESH,
        )
        c.start()
        sends.append(c)

    def agy2(u):
        for hf, dev, dev2 in ((0, dev_y3, dev_y1), (1, dev_y1, dev_y3)):
            o = 4 * f1[hf] + 2 * (1 - f2[hf])
            wait(f"g1{u}.{hf}", c1all.at[u, hf, pl.ds(o, 2)])
            slot = c1all.at[u, hf, pl.ds(4 * f1[hf], 4)]
            send(f"g2{u}.{hf}", slot, slot, dev2)

    def mmt(u):
        for hf in range(2):
            wait(f"g2{u}.{hf}", c1all.at[u, hf, pl.ds(4 * (1 - f1[hf]), 4)])
        for half in range(2):
            split_half(c1all, u, half, cs_ref, KR)
        lhs = cs_ref[...]

        @pl.loop(0, 7)
        def _(j):
            c0 = pl.multiple_of(j * 256, 256)
            r = lax.dot_general(lhs, hhi[:, pl.ds(c0, 256)], NN, preferred_element_type=F32)
            r2 = lax.dot_general(lhs[:128], hlo[:, pl.ds(c0, 256)], NN, preferred_element_type=F32)
            qbuf[u, :, :, :, pl.ds(c0, 256)] = (r[:128] + r[128:] + r2).reshape(2, 8, 8, 256)

        for o in (4, -3, 3, -2, 2, -1, 1, 0):
            send(f"y{u}.{o}", qbuf.at[u, xo, zi(o), :, LO], rx1.at[u, zi(o)], dev_x)
        hi_of = lambda o: qbuf.at[u, xo, zi(o), :, HI]
        send(f"ha{u}.1", hi_of(3), rpa.at[u, 0], dev_a)
        send(f"hb{u}.1", hi_of(-4), rpb.at[u, 0], dev_b)

    def rsum(u, s):
        def take_x(o):
            wait(f"y{u}.{o}", rx1.at[u, zi(o)])
            qbuf[u, x, zi(o), :, LO] = qbuf[u, x, zi(o), :, LO] + rx1[u, zi(o)]

        def add(o, buf, j):
            qbuf[u, x, zi(o)] = qbuf[u, x, zi(o)] + buf[u, j]

        def addh(o, buf, j):
            qbuf[u, xo, zi(o), :, HI] = qbuf[u, xo, zi(o), :, HI] + buf[u, j]

        if s <= 4:
            o = 5 - s
            take_x(o)
            if s > 1:
                wait(f"za{u}.{s - 1}", rza.at[u, s - 2])
                add(o, rza, s - 2)
            send(f"za{u}.{s}", qbuf.at[u, x, zi(o)], rza.at[u, s - 1], dev_a)
        if s <= 3:
            o = -(4 - s)
            take_x(o)
            if s > 1:
                wait(f"zb{u}.{s - 1}", rzb.at[u, s - 2])
                add(o, rzb, s - 2)
            send(f"zb{u}.{s}", qbuf.at[u, x, zi(o)], rzb.at[u, s - 1], dev_b)
        if s <= 3:
            wait(f"ha{u}.{s}", rpa.at[u, s - 1])
            o = 3 - s
            addh(o, rpa, s - 1)
            if s < 3:
                send(f"ha{u}.{s + 1}", qbuf.at[u, xo, zi(o), :, HI], rpa.at[u, s], dev_a)
        if s <= 4:
            wait(f"hb{u}.{s}", rpb.at[u, s - 1])
            o = -(4 - s)
            addh(o, rpb, s - 1)
            if s < 4:
                send(f"hb{u}.{s + 1}", qbuf.at[u, xo, zi(o), :, HI], rpb.at[u, s], dev_b)
            else:
                send(f"xf{u}", qbuf.at[u, xo, z, :, HI], rxf.at[u], dev_x)
        if s == 5:
            take_x(0)
            wait(f"zb{u}.3", rzb.at[u, 2])
            wait(f"za{u}.4", rza.at[u, 3])
            wait(f"xf{u}", rxf.at[u])
            v = qbuf[u, x, z] + rza[u, 3] + rzb[u, 2]
            g1_out[u, :, LO] = v[:, :KR]
            g1_out[u, :, HI] = v[:, KR:] + rxf[u]
            for h in range(2):
                n0 = sem(f"c{u}.0r") + h
                pltpu.make_async_remote_copy(
                    src_ref=ch.at[u, h], dst_ref=ch.at[u, h], send_sem=ss.at[n0], recv_sem=rs.at[n0],
                    device_id=dev_x, device_id_type=MESH,
                ).wait_recv()
                c1_out[u, :, pl.ds(h * KR, KR)] = ch[u, h]

    for u in range(U):
        for i in range(2):
            sem(f"a{u}.{i}")
        sem(f"c{u}.0r")
        sem(f"c{u}.1r")

    def relay_send(u):
        for h in range(2):
            n0 = sem(f"as{u}.{h}")
            c = pltpu.make_async_remote_copy(
                src_ref=a_ref.at[u, :, pl.ds(h * KR, KR)], dst_ref=ab.at[u, z % 2],
                send_sem=ss.at[n0], recv_sem=rs.at[sem(f"a{u}.0") + z % 2],
                device_id=dev_out[h], device_id_type=MESH,
            )
            c.start()
            sends.append(c)

    start_h()
    for t, u, name, s in SCHEDULE:
        if name == "ag":
            ag(u, s)
            if s == 1:
                relay_send(u)
            if u == 0 and s == 1:
                hcopy.wait()
                split_rows(k)
            if u == 0 and s == 3:
                wait("h", hbuf.at[1 - k])
                split_rows(1 - k)
        elif name == "rs":
            rsum(u, s)
        else:
            {"mm": mm, "rsy2": rsy2, "xhi": xhi, "agy1": agy1, "agy2": agy2, "mmt": mmt}[name](u)
    for c in sends:
        c.wait_send()
    assert len(names) <= NSEM, len(names)


NSEM = 320


def run_kernel(h, c0, a):
    v = pltpu.VMEM
    scratch = [
        v((2, 448, KC), F32), v((KR, KC), BF16), v((KR, KC), BF16), v((256, KC), BF16),
        v((U, 2, 8, 8, KC), F32),
        v((U, 2, 8, 8, KR), F32),
        v((U, 2, 4, 8, KR), F32), v((U, 2, 2, 8, KR), F32),
        v((U, 2, 2, 8, KR), F32), v((U, 2, 2, 8, KR), F32),
        v((U, 2, 8, 8, KR), F32), v((256, KR), BF16),
        v((U, 2, 8, 8, KC), F32),
        v((U, 8, 8, KR), F32),
        v((U, 4, 8, KC), F32), v((U, 3, 8, KC), F32),
        v((U, 3, 8, KR), F32), v((U, 4, 8, KR), F32),
        v((U, 8, KR), F32),
        v((U, 2, 8, KR), F32), v((U, 2, 8, KR), F32),
        pltpu.SemaphoreType.DMA((NSEM,)), pltpu.SemaphoreType.DMA((NSEM,)),
        pltpu.SemaphoreType.DMA((1,)),
    ]
    return pl.pallas_call(
        kernel,
        out_shape=[jax.ShapeDtypeStruct((U, 8, KC), F32)] * 2,
        in_specs=[pl.BlockSpec(memory_space=pl.ANY)] + [pl.BlockSpec(memory_space=pltpu.VMEM)] * 2,
        out_specs=[pl.BlockSpec(memory_space=pltpu.VMEM)] * 2,
        scratch_shapes=scratch,
        compiler_params=pltpu.CompilerParams(
            collective_id=0, has_side_effects=True, vmem_limit_bytes=56 * 1024 * 1024
        ),
    )(h, c0, a)


def per_device(hessian, dense_weight, start_iterate, start_multiplier, keep_mask):
    weight, iterate0, multiplier0 = dense_weight.T, start_iterate.T, start_multiplier.T
    keeping = keep_mask.T.astype(F32)
    projected0 = keeping * (iterate0 + multiplier0)
    change = iterate0 - weight
    start = change - STEP * (iterate0 - projected0 + multiplier0)
    c1, g1 = run_kernel(hessian, change.reshape(U, 8, KC), start.reshape(U, 8, KC))
    iterate1 = c1.reshape(32, KC) + weight
    projected1 = keeping * (iterate1 + multiplier0)
    multiplier1 = multiplier0 + iterate1 - projected1
    iterate2 = iterate1 - STEP * (g1.reshape(32, KC) + (iterate1 - projected1 + multiplier1))
    projected2 = keeping * (iterate2 + multiplier1)
    multiplier2 = multiplier1 + iterate2 - projected2
    return iterate2.T, projected2.T, multiplier2.T


def solution(mesh):
    return jax.shard_map(
        per_device,
        mesh=mesh,
        in_specs=(P("row", "col"),) + (P("col", "row"),) * 4,
        out_specs=(P("col", "row"),) * 3,
        check_vma=False,
    )
```

time: 364 us -> 156 us (0.43)
  Pallas kernels: 0 us -> 151 us
  waiting for transfers between devices: 140 us -> 0 us
  blocking collectives: 125 us -> 0 us
  local copies, waits for them, and re-layouts: 29.9 us -> 0.01 us
  matrix products: 25.8 us -> 0 us
  other arithmetic: 28.2 us -> 4.16 us
  between operations: 14.1 us -> 0.69 us
    pallas_call x0 -> x1, Pallas kernels: none -> 151 us  [run_kernel(): pl.pallas_call(kernel, out_shape=[jax.ShapeDtypeStruct((U, 8, KC), F32)]...]
    all_gather x2 -> x0, waiting for transfers between devices: 140 us -> none  [per_device(): gathered = lax.all_gather(change, 'row', axis=1, tiled=True)]
    all_to_all x6 -> x0, blocking collectives: 125 us -> none  [the longest x2 62.8 us: sum_at_owner(): lax.all_to_all(tiles, axis, split_axis=0, concat_axis=0, tiled=True)]
    dot_general x2 -> x0, matrix products: 25.8 us -> none  [per_device(): jnp.dot(hessian, gathered, precision=lax.Precision.HIGHEST, preferred_ele...]
    unnamed x15 -> x6, local copies, waits for them, and re-layouts: 19.6 us -> 0.01 us
    all_to_all x4 -> x0, other arithmetic: 11.3 us -> none  [the longest x2 5.63 us: per_device(): lax.all_to_all(shaped, 'row', split_axis=3, concat_axis=0, tiled=True)]
    unnamed x2 -> x0, other arithmetic: 7.59 us -> none
    sub x3 -> x0, other arithmetic: 6.13 us -> none  [the longest x2 4.03 us: per_device(): change = iterate - dense_weight]
  transfers between devices with their start and end apart: 2 -> 0, of which waited for: 2 -> 0; matrix products, arithmetic and copies ran while one was open for 0% -> 0% of each run, Pallas kernels for 0% -> 0%
where the time goes in v1:
time: 156 us
  Pallas kernels  151 us (97%)
  other arithmetic  4.16 us (3%)
    pallas_call x1, Pallas kernels, run_kernel(): pl.pallas_call(kernel, out_shape=[jax.ShapeDtypeStruct((U, 8, KC), F32)]...  151 us

profile of v1, /device:TPU:8, one launch (start us, length us, event | category | flops | bytes accessed | tf_op | source)
XLA Modules:
  0.0 156.1 jit_solution(13234639501230932587)
XLA Ops:
  0.6 0.0 copy-start
  0.6 0.0 copy-start.1
  0.7 0.0 copy-start.2
  0.7 2.2 %fusion.6 = (f32[4,8,1792]{2,1,0:T(8,128)}, f32[4,8,1792]{2,1,0:T(8,128)}) fusion(f32[1792,32]{0,1:T(8,128)} %param.8, f32[1792,32]{0,1:T(8,128)} %param.7, s32[1792,32]{0,1:T(8,128)} %param.9, f32[1792,32]{0,1:T(8,128)} %param.6), kind=kLoop, calls=%fused_computation.11 | loop fusion | flops 458752 | bytes 1376256 | tf_op jit(solution)/shard_map/reshape | solution.py:424
  2.8 151.2 %shard_map.76 = (f32[4,8,1792]{2,1,0:T(8,128)}, f32[4,8,1792]{2,1,0:T(8,128)}) custom-call(f32[448,1792]{1,0:T(8,128)} %h_ref.1, f32[4,8,1792]{2,1,0:T(8,128)} %get-tuple-element.11.c0_ref, f32[4,8,1792]{2,1,0:T(8,128)} %get-tuple-element.10.a_ref), custom_call_target="tpu_custom_call" | custom-call | tf_op jit(solution)/shard_map/pallas_call | solution.py:406
  154.1 0.0 copy-done
  154.1 0.0 copy-done.1
  154.1 0.0 copy-done.2
  154.1 2.0 %subtract_bitcast_fusion = (f32[1792,32]{0,1:T(8,128)}, f32[1792,32]{0,1:T(8,128)}, f32[1792,32]{0,1:T(8,128)}) fusion(s32[1792,32]{0,1:T(8,128)S(1)} %copy-done, f32[1792,32]{0,1:T(8,128)S(1)} %copy-done.1, f32[4,8,1792]{2,1,0:T(8,128)} %get-tuple-element.6, f32[1792,32]{0,1:T(8,128)S(1)} %copy-done.2, f32[4,8,1792]{2,1,0:T(8,128)} %get-tuple-element.5), kind=kLoop, calls=%fused_computation.15 | loop fusion | flops 745472 | bytes 1835008 | tf_op jit(solution)/shard_map/transpose | solution.py:431
Async XLA Ops:
  0.6 153.4 %copy-start = (s32[1792,32]{0,1:T(8,128)S(1)}, s32[1792,32]{0,1:T(8,128)}, u32[]{:S(2)}) copy-start(s32[1792,32]{0,1:T(8,128)} %param.9) | copy-start | bytes 688132
  0.6 153.4 %copy-start.1 = (f32[1792,32]{0,1:T(8,128)S(1)}, f32[1792,32]{0,1:T(8,128)}, u32[]{:S(2)}) copy-start(f32[1792,32]{0,1:T(8,128)} %param.8) | copy-start | bytes 688132
  0.7 153.4 %copy-start.2 = (f32[1792,32]{0,1:T(8,128)S(1)}, f32[1792,32]{0,1:T(8,128)}, u32[]{:S(2)}) copy-start(f32[1792,32]{0,1:T(8,128)} %param.6) | copy-start | bytes 688132

commit v2 on v0

v2 whole, which is shorter than its diff:
```python
import jax
import jax.numpy as jnp
from jax import lax
from jax.experimental import pallas as pl
from jax.experimental.pallas import tpu as pltpu
from jax.sharding import PartitionSpec as P

MESH = pl.DeviceIdType.MESH
STEP = 0.25
U = 4
KC = 1792
KR = 896
F32 = jnp.float32
BF16 = jnp.bfloat16


ORDER = (
    ("ag0", 1, 0), ("ag0", 2, 0), ("ag0", 3, 0), ("gx", 0, 0), ("rel", 0, 0), ("ga", 0, 1), ("gb", 0, 1),
    ("gx", 1, 0), ("rel", 1, 0), ("gb", 1, 1), ("ga", 1, 1), ("gx", 2, 0), ("rel", 2, 0), ("ga", 2, 1),
    ("gb", 2, 1), ("gx", 3, 0), ("rel", 3, 0), ("gb", 3, 1), ("ga", 3, 1), ("gpb", 0, 1), ("gpa", 0, 1),
    ("gb", 0, 2), ("ga", 0, 2), ("gpa", 1, 1), ("gpb", 1, 1), ("ga", 1, 2), ("gb", 1, 2), ("gpb", 2, 1),
    ("gpa", 2, 1), ("ga", 2, 2), ("gb", 2, 2), ("gpb", 3, 1), ("gpa", 3, 1), ("ga", 3, 2), ("gb", 3, 2),
    ("gpa", 0, 2), ("gpb", 0, 2), ("ga", 0, 3), ("gb", 0, 3), ("gpb", 1, 2), ("gpa", 1, 2), ("ga", 1, 3),
    ("gb", 1, 3), ("gpb", 2, 2), ("gpa", 2, 2), ("gb", 2, 3), ("ga", 2, 3), ("gpb", 3, 2), ("gpa", 3, 2),
    ("ga", 3, 3), ("gb", 3, 3), ("rel2", 0, 0), ("rel2", 1, 0), ("gpb", 0, 3), ("rel2", 2, 0), ("rel2", 3, 0),
    ("gpb", 1, 3), ("ga", 0, 4), ("gpb", 2, 3), ("gpb", 3, 3), ("ga", 1, 4), ("mm", 0, 0), ("ga", 2, 4),
    ("ga", 3, 4), ("mm", 0, 1), ("mm", 1, 0), ("mm", 1, 1), ("mm", 2, 0), ("ry", 0, 0), ("ry", 0, 1),
    ("mm", 2, 1), ("mm", 3, 0), ("ry", 1, 1), ("ry", 1, 0), ("xhi", 0, 0), ("mm", 3, 1), ("ry", 2, 1),
    ("ry", 2, 0), ("xhi", 1, 0), ("ay1", 0, 0), ("ry", 3, 1), ("ry", 3, 0), ("xhi", 2, 0), ("ay2", 0, 0),
    ("ay2", 0, 1), ("ay1", 1, 0), ("xhi", 3, 0), ("crel", 0, 0), ("ay1", 2, 0), ("mmt", 0, 0), ("ay2", 1, 1),
    ("ay2", 1, 0), ("crel", 1, 0), ("ay1", 3, 0), ("ay2", 2, 0), ("ay2", 2, 1), ("mmt", 0, 1), ("ra", 0, 1),
    ("rb", 0, 1), ("crel", 2, 0), ("mmt", 1, 0), ("rpa", 0, 1), ("rpb", 0, 1), ("ra", 0, 2), ("rb", 0, 2),
    ("ay2", 3, 0), ("ay2", 3, 1), ("crel", 3, 0), ("mmt", 1, 1), ("ra", 1, 1), ("mmt", 2, 0), ("rpa", 0, 2),
    ("rpb", 0, 2), ("ra", 0, 3), ("rb", 0, 3), ("rb", 1, 1), ("rpa", 1, 1), ("rpb", 1, 1), ("mmt", 2, 1),
    ("ra", 1, 2), ("mmt", 3, 0), ("rpb", 0, 3), ("ra", 0, 4), ("ra", 2, 1), ("rpa", 1, 2), ("rb", 2, 1),
    ("rpa", 2, 1), ("rb", 1, 2), ("mmt", 3, 1), ("rpb", 1, 2), ("rpf", 0, 0), ("ra", 1, 3), ("rpb", 2, 1),
    ("ra", 3, 1), ("rb", 3, 1), ("rb", 2, 2), ("ra", 2, 2), ("rb", 1, 3), ("rpa", 2, 2), ("rpb", 3, 1),
    ("rpb", 1, 3), ("rpa", 3, 1), ("rpb", 2, 2), ("fin", 0, 0), ("ra", 1, 4), ("rb", 3, 2), ("ra", 3, 2),
    ("rb", 2, 3), ("ra", 2, 3), ("rpa", 3, 2), ("rpb", 3, 2), ("rpf", 1, 0), ("rpb", 2, 3), ("ra", 3, 3),
    ("rb", 3, 3), ("fin", 1, 0), ("ra", 2, 4), ("rpb", 3, 3), ("rpf", 2, 0), ("ra", 3, 4), ("fin", 2, 0),
    ("rpf", 3, 0), ("fin", 3, 0),
)


def kernel(
    h_ref, w_ref, i_ref, m_ref, k_ref, c1_out, g1_out,
    wv, iv, mv, kv, c0_ref, a_ref,
    hbuf, hhi, hlo, xs_ref, xall, pbuf, rb1, rb2, vbuf, xb, c1all, cs_ref, qbuf,
    rx1, rza, rzb, rpa, rpb, rxf, ab, ch, ai, ci, ss, rs, hs,
):
    row = lax.axis_index("row")
    col = lax.axis_index("col")
    k = row % 2
    z = (row // 2) % 8
    x = row // 16
    y = col // 2
    xh = col % 2
    d = 1 - 2 * k
    xo = 1 - x

    def zi(off):
        return (z + d * off + 16) % 8

    def dev_z(off):
        return (x * 16 + zi(off) * 2 + k, col)

    dev_a, dev_b = dev_z(1), dev_z(-1)
    dev_x = (xo * 16 + z * 2 + k, col)
    dev_core = (x * 16 + z * 2 + (1 - k), col)
    y1 = y + 1 - 2 * (y % 2)
    y3 = 3 - y
    dev_y1 = (row, y1 * 2 + xh)
    dev_y3 = (row, y3 * 2 + xh)
    dev_xh = (row, y * 2 + (1 - xh))

    b0, b1 = y % 2, y // 2
    bx = (b0 + b1) % 2
    m0, m1 = (z // 2) % 2, z // 4
    f1 = ((bx + m1) % 2, (b1 + m1) % 2)
    f2 = ((1 - b1 + m0) % 2, (1 - b0 + m0) % 2)
    q = (2 * f1[0] + f2[0], 2 * f1[1] + f2[1])
    q0 = (2 * bx + 1 - b1, 2 * b1 + 1 - b0)

    cblk = y * 2 + xh
    e0, e1 = (z // 2 + cblk) % 2, (z // 4 + (cblk % 4) // 2) % 2
    ya_b1 = 1 - e0
    ya_b0 = (e1 + ya_b1) % 2
    y_if0 = 2 * ya_b1 + ya_b0
    y_if1 = 2 * e1 + (1 - e0)
    yd = (1 - x) * y_if0 + x * y_if1
    md = 2 * ((q0[1] // 2) * xh + (q0[0] // 2) * (1 - xh) + z // 4 - 2 * (((q0[1] // 2) * xh + (q0[0] // 2) * (1 - xh)) * (z // 4)))
    t0 = (q0[1] % 2) * xh + (q0[0] % 2) * (1 - xh)
    md = md + t0 + (z // 2) % 2 - 2 * (t0 * ((z // 2) % 2))
    dev_mid = ((y // 2) * 16 + z * 2 + k, yd * 2 + x)
    dev_home = (xh * 16 + z * 2 + k, 4 * x + md)
    dev_zz = [(x * 16 + (2 * md + h) * 2 + k, col) for h in range(2)]

    def here(dev):
        return jnp.logical_and(dev[0] == row, dev[1] == col)

    hpart = z % 2

    barrier = pltpu.get_barrier_semaphore()
    peers = [dev_a, dev_b, dev_x, dev_core, dev_y1, dev_y3, dev_xh]
    for p in peers:
        pl.semaphore_signal(barrier, inc=1, device_id=p, device_id_type=MESH)
    expected = len(peers)
    for p in [dev_mid, dev_home] + dev_zz:
        same = here(p)
        expected = expected + 1 - same.astype(jnp.int32)

        @pl.when(jnp.logical_not(same))
        def _():
            pl.semaphore_signal(barrier, inc=1, device_id=p, device_id_type=MESH)

    loads = [
        pltpu.make_async_copy(src, dst, hs.at[n])
        for n, (src, dst) in enumerate(((w_ref, wv), (i_ref, iv), (m_ref, mv), (k_ref, kv), (h_ref, hbuf.at[k])))
    ]
    for c in loads:
        c.start()
    loads[0].wait()
    loads[1].wait()
    for u in range(U):
        c0_ref[u] = iv[u] - wv[u]
    loads[2].wait()
    loads[3].wait()
    for u in range(U):
        v0, m0 = iv[u], mv[u]
        p0 = kv[u].astype(F32) * (v0 + m0)
        a_ref[u] = c0_ref[u] - STEP * (v0 - p0 + m0)
        xall[u, x, z] = c0_ref[u]

    names = {}
    sends = []
    moves = []

    def sem(name):
        return names.setdefault(name, len(names))

    def send(name, src, dst, dev):
        i = sem(name)
        c = pltpu.make_async_remote_copy(
            src_ref=src, dst_ref=dst, send_sem=ss.at[i], recv_sem=rs.at[i],
            device_id=dev, device_id_type=MESH,
        )
        c.start()
        sends.append(c)

    def move(name, recv, src, dst, dev):
        i = sem(name)
        same = here(dev)
        c = pltpu.make_async_remote_copy(
            src_ref=src, dst_ref=dst, send_sem=ss.at[i], recv_sem=rs.at[recv],
            device_id=dev, device_id_type=MESH,
        )

        @pl.when(jnp.logical_not(same))
        def _():
            c.start()

        @pl.when(same)
        def _():
            pltpu.make_async_copy(src, dst, rs.at[recv]).start()

        moves.append((c, same))

    def wait(name, slot):
        i = sem(name)
        pltpu.make_async_remote_copy(
            src_ref=slot, dst_ref=slot, send_sem=ss.at[i], recv_sem=rs.at[i],
            device_id=dev_x, device_id_type=MESH,
        ).wait_recv()

    LO = pl.ds(0, KR)
    HI = pl.ds(KR, KR)

    def split_rows(part):
        @pl.loop(0, 28)
        def _(i):
            r0 = pl.multiple_of(i * 16, 16)
            v = hbuf[part, pl.ds(r0, 16), :]
            hi = v.astype(BF16)
            o0 = pl.multiple_of(part * 448 + i * 16, 16)
            hhi[pl.ds(o0, 16), :] = hi
            hlo[pl.ds(o0, 16), :] = (v - hi.astype(F32)).astype(BF16)

    def full(u, o):
        return xall.at[u, x, zi(o)]

    def par(u, o):
        return xall.at[u, xo, zi(o), :, HI]

    def low(u, o):
        return xall.at[u, x, zi(o), :, LO]

    def ag0(u, s):
        send(f"fa{u}.1", c0_ref.at[u], full(u, 0), dev_a)
        send(f"fb{u}.1", c0_ref.at[u], full(u, 0), dev_b)
        send(f"x{u}", c0_ref.at[u], full(u, 0), dev_x)

    def ga(u, s):
        wait(f"fa{u}.{s}", full(u, -s))
        if s < 4:
            send(f"fa{u}.{s + 1}", full(u, -s), full(u, -s), dev_a)
        send(f"xa{u}.{s}", low(u, -s), low(u, -s), dev_x)

    def gb(u, s):
        wait(f"fb{u}.{s}", full(u, s))
        if s < 3:
            send(f"fb{u}.{s + 1}", full(u, s), full(u, s), dev_b)
        send(f"xb{u}.{s}", low(u, s), low(u, s), dev_x)

    def gx(u, s):
        wait(f"x{u}", xall.at[u, xo, z])
        send(f"pa{u}.1", par(u, 0), par(u, 0), dev_a)
        send(f"pb{u}.1", par(u, 0), par(u, 0), dev_b)

    def gpa(u, s):
        wait(f"pa{u}.{s}", par(u, -s))
        send(f"pa{u}.{s + 1}", par(u, -s), par(u, -s), dev_a)

    def gpb(u, s):
        wait(f"pb{u}.{s}", par(u, s))
        send(f"pb{u}.{s + 1}", par(u, s), par(u, s), dev_b)

    def wait_gather(u):
        wait(f"pa{u}.3", par(u, -3))
        wait(f"pb{u}.4", par(u, 4))
        olow = lambda o: xall.at[u, xo, zi(o), :, LO]
        for j in range(1, 5):
            wait(f"xa{u}.{j}", olow(-j))
        for j in range(1, 4):
            wait(f"xb{u}.{j}", olow(j))

    NT = (((1,), (1,)), ((), ()))
    NN = (((1,), (0,)), ((), ()))

    def mm_part(u, c0, n):
        r = lax.dot_general(xs_ref[...], hhi[pl.ds(c0, n), :], NT, preferred_element_type=F32)
        r2 = lax.dot_general(xs_ref[:128], hlo[pl.ds(c0, n), :], NT, preferred_element_type=F32)
        v = (r[:128] + r[128:] + r2) * (-STEP)
        pbuf[u, :, :, :, pl.ds(c0, n)] = v.reshape(2, 8, 8, n)

    def mm(u, s):
        if s == 0:
            wait_gather(u)
            if u == 0:
                wait("h", hbuf.at[1 - k])
                split_rows(1 - k)
            for half in range(2):
                split_half(xall, u, half, xs_ref, KC)

            @pl.loop(0, 2)
            def _(j):
                mm_part(u, pl.multiple_of(j * 256, 256), 256)

            return
        mm_part(u, 512, 256)
        mm_part(u, 768, 128)
        send(f"r1{u}.0", pbuf.at[u, 0, pl.ds(4 * (1 - f1[0]), 4)], rb1.at[u, 0], dev_y1)
        send(f"r1{u}.1", pbuf.at[u, 1, pl.ds(4 * (1 - f1[1]), 4)], rb1.at[u, 1], dev_y3)

    def split_half(src, u, half, dst, width):
        @pl.loop(0, 4)
        def _(i):
            v = src[u, half, pl.ds(i * 2, 2)].reshape(16, width)
            hi = v.astype(BF16)
            r0 = half * 64 + i * 16
            dst[pl.ds(pl.multiple_of(r0, 16), 16), :] = hi
            dst[pl.ds(pl.multiple_of(128 + r0, 16), 16), :] = (v - hi.astype(F32)).astype(BF16)

    def ry(u, hf):
        dev2 = (dev_y3, dev_y1)[hf]
        wait(f"r1{u}.{hf}", rb1.at[u, hf])
        base = 4 * f1[hf]
        o = 2 * (1 - f2[hf])
        pbuf[u, hf, pl.ds(base + o, 2)] = pbuf[u, hf, pl.ds(base + o, 2)] + rb1[u, hf, pl.ds(o, 2)]
        send(f"r2{u}.{hf}", pbuf.at[u, hf, pl.ds(base + o, 2)], rb2.at[u, hf], dev2)
        o = 2 * f2[hf]
        vbuf[u, hf] = pbuf[u, hf, pl.ds(base + o, 2)] + rb1[u, hf, pl.ds(o, 2)]

    def xhi(u, s):
        for i in range(2):
            wait(f"a{u}.{i}", ab.at[u, i])
        vbuf[u, xh] = vbuf[u, xh] + ab[u]
        for hf in range(2):
            wait(f"r2{u}.{hf}", rb2.at[u, hf])
            vbuf[u, hf] = vbuf[u, hf] + rb2[u, hf]
        send(f"xh{u}", vbuf.at[u], xb.at[u], dev_xh)

    def ay1(u, s):
        wait(f"xh{u}", xb.at[u])
        for hf, dev in ((0, dev_y3), (1, dev_y1)):
            slot = c1all.at[u, hf, pl.ds(2 * q[hf], 2)]
            c1all[u, hf, pl.ds(2 * q[hf], 2)] = vbuf[u, hf] + xb[u, hf]
            send(f"g1{u}.{hf}", slot, slot, dev)
        for i in range(2):
            move(f"cs{u}.{i}", sem(f"c{u}.0") + hpart, c1all.at[u, xh, 2 * md + i], ci.at[u, hpart], dev_zz[i])

    def rel(u, s):
        move(f"as{u}", sem(f"am{u}"), a_ref.at[u], ai.at[u], dev_mid)

    def rel2(u, s):
        wait(f"am{u}", ai.at[u])
        for h in range(2):
            src = ai.at[u, :, pl.ds(h * KR, KR)]
            move(f"at{u}.{h}", sem(f"a{u}.0") + hpart, src, ab.at[u, hpart], dev_zz[h])

    def crel(u, s):
        for h in range(2):
            wait(f"c{u}.{h}", ci.at[u, h])
        move(f"ct{u}", sem(f"ch{u}"), ci.at[u], ch.at[u], dev_home)

    def ay2(u, hf):
        dev2 = (dev_y1, dev_y3)[hf]
        o = 4 * f1[hf] + 2 * (1 - f2[hf])
        wait(f"g1{u}.{hf}", c1all.at[u, hf, pl.ds(o, 2)])
        slot = c1all.at[u, hf, pl.ds(4 * f1[hf], 4)]
        send(f"g2{u}.{hf}", slot, slot, dev2)

    def mmt_part(u, c0, n):
        r = lax.dot_general(cs_ref[...], hhi[:, pl.ds(c0, n)], NN, preferred_element_type=F32)
        r2 = lax.dot_general(cs_ref[:128], hlo[:, pl.ds(c0, n)], NN, preferred_element_type=F32)
        qbuf[u, :, :, :, pl.ds(c0, n)] = (r[:128] + r[128:] + r2).reshape(2, 8, 8, n)

    def mmt(u, s):
        if s == 0:
            for hf in range(2):
                wait(f"g2{u}.{hf}", c1all.at[u, hf, pl.ds(4 * (1 - f1[hf]), 4)])
            for half in range(2):
                split_half(c1all, u, half, cs_ref, KR)

            @pl.loop(0, 4)
            def _(j):
                mmt_part(u, pl.multiple_of(j * 256, 256), 256)

            for o in (4, -3, 3, -2, 2, -1, 1, 0):
                send(f"y{u}.{o}", qbuf.at[u, xo, zi(o), :, LO], rx1.at[u, zi(o)], dev_x)
            return

        @pl.loop(4, 7)
        def _(j):
            mmt_part(u, pl.multiple_of(j * 256, 256), 256)

        send(f"ha{u}.1", qbuf.at[u, xo, zi(3), :, HI], rpa.at[u, 0], dev_a)
        send(f"hb{u}.1", qbuf.at[u, xo, zi(-4), :, HI], rpb.at[u, 0], dev_b)

    def take_x(u, o):
        wait(f"y{u}.{o}", rx1.at[u, zi(o)])
        qbuf[u, x, zi(o), :, LO] = qbuf[u, x, zi(o), :, LO] + rx1[u, zi(o)]

    def add(u, o, buf, j):
        qbuf[u, x, zi(o)] = qbuf[u, x, zi(o)] + buf[u, j]

    def addh(u, o, buf, j):
        qbuf[u, xo, zi(o), :, HI] = qbuf[u, xo, zi(o), :, HI] + buf[u, j]

    def ra(u, s):
        o = 5 - s
        take_x(u, o)
        if s > 1:
            wait(f"za{u}.{s - 1}", rza.at[u, s - 2])
            add(u, o, rza, s - 2)
        send(f"za{u}.{s}", qbuf.at[u, x, zi(o)], rza.at[u, s - 1], dev_a)

    def rb(u, s):
        o = -(4 - s)
        take_x(u, o)
        if s > 1:
            wait(f"zb{u}.{s - 1}", rzb.at[u, s - 2])
            add(u, o, rzb, s - 2)
        send(f"zb{u}.{s}", qbuf.at[u, x, zi(o)], rzb.at[u, s - 1], dev_b)

    def rpa_(u, s):
        wait(f"ha{u}.{s}", rpa.at[u, s - 1])
        o = 3 - s
        addh(u, o, rpa, s - 1)
        if s < 3:
            send(f"ha{u}.{s + 1}", qbuf.at[u, xo, zi(o), :, HI], rpa.at[u, s], dev_a)

    def rpb_(u, s):
        wait(f"hb{u}.{s}", rpb.at[u, s - 1])
        o = -(4 - s)
        addh(u, o, rpb, s - 1)
        if s < 4:
            send(f"hb{u}.{s + 1}", qbuf.at[u, xo, zi(o), :, HI], rpb.at[u, s], dev_b)

    def rpf(u, s):
        rpa_(u, 3)
        rpb_(u, 4)
        send(f"xf{u}", qbuf.at[u, xo, z, :, HI], rxf.at[u], dev_x)

    def fin(u, s):
        take_x(u, 0)
        wait(f"zb{u}.3", rzb.at[u, 2])
        wait(f"za{u}.4", rza.at[u, 3])
        wait(f"xf{u}", rxf.at[u])
        v = qbuf[u, x, z] + rza[u, 3] + rzb[u, 2]
        g1_out[u, :, LO] = v[:, :KR]
        g1_out[u, :, HI] = v[:, KR:] + rxf[u]
        wait(f"ch{u}", ch.at[u])
        for h in range(2):
            c1_out[u, :, pl.ds(h * KR, KR)] = ch[u, h]

    for u in range(U):
        for i in range(2):
            sem(f"a{u}.{i}")
        for i in range(2):
            sem(f"c{u}.{i}")

    stages = dict(
        ag0=ag0, ga=ga, gb=gb, gx=gx, gpa=gpa, gpb=gpb, mm=mm, ry=ry, xhi=xhi, ay1=ay1, ay2=ay2,
        mmt=mmt, ra=ra, rb=rb, rpa=rpa_, rpb=rpb_, rpf=rpf, fin=fin, rel=rel, rel2=rel2, crel=crel,
    )
    pl.semaphore_wait(barrier, expected)
    ag0(0, 0)
    loads[4].wait()
    send("h", h_ref, hbuf.at[k], dev_core)
    split_rows(k)
    for name, u, s in ORDER:
        stages[name](u, s)
    for c in sends:
        c.wait_send()
    for c, same in moves:

        @pl.when(jnp.logical_not(same))
        def _():
            c.wait_send()

    assert len(names) <= NSEM, len(names)


NSEM = 320


def run_kernel(h, *arrays):
    v = pltpu.VMEM
    scratch = [
        v((U, 8, KC), F32), v((U, 8, KC), F32), v((U, 8, KC), F32), v((U, 8, KC), jnp.int32),
        v((U, 8, KC), F32), v((U, 8, KC), F32),
        v((2, 448, KC), F32), v((KR, KC), BF16), v((KR, KC), BF16), v((256, KC), BF16),
        v((U, 2, 8, 8, KC), F32),
        v((U, 2, 8, 8, KR), F32),
        v((U, 2, 4, 8, KR), F32), v((U, 2, 2, 8, KR), F32),
        v((U, 2, 2, 8, KR), F32), v((U, 2, 2, 8, KR), F32),
        v((U, 2, 8, 8, KR), F32), v((256, KR), BF16),
        v((U, 2, 8, 8, KC), F32),
        v((U, 8, 8, KR), F32),
        v((U, 4, 8, KC), F32), v((U, 3, 8, KC), F32),
        v((U, 3, 8, KR), F32), v((U, 4, 8, KR), F32),
        v((U, 8, KR), F32),
        v((U, 2, 8, KR), F32), v((U, 2, 8, KR), F32),
        v((U, 8, KC), F32), v((U, 2, 8, KR), F32),
        pltpu.SemaphoreType.DMA((NSEM,)), pltpu.SemaphoreType.DMA((NSEM,)),
        pltpu.SemaphoreType.DMA((5,)),
    ]
    return pl.pallas_call(
        kernel,
        out_shape=[jax.ShapeDtypeStruct((U, 8, KC), F32)] * 2,
        in_specs=[pl.BlockSpec(memory_space=pl.ANY)] * 5,
        out_specs=[pl.BlockSpec(memory_space=pltpu.VMEM)] * 2,
        scratch_shapes=scratch,
        compiler_params=pltpu.CompilerParams(
            collective_id=0, has_side_effects=True, vmem_limit_bytes=56 * 1024 * 1024
        ),
    )(h, *(t.reshape(U, 8, KC) for t in arrays))


def per_device(hessian, dense_weight, start_iterate, start_multiplier, keep_mask):
    weight, iterate0, multiplier0 = dense_weight.T, start_iterate.T, start_multiplier.T
    keeping = keep_mask.T.astype(F32)
    c1, g1 = run_kernel(hessian, weight, iterate0, multiplier0, keep_mask.T)
    iterate1 = c1.reshape(32, KC) + weight
    projected1 = keeping * (iterate1 + multiplier0)
    multiplier1 = multiplier0 + iterate1 - projected1
    iterate2 = iterate1 - STEP * (g1.reshape(32, KC) + (iterate1 - projected1 + multiplier1))
    projected2 = keeping * (iterate2 + multiplier1)
    multiplier2 = multiplier1 + iterate2 - projected2
    return iterate2.T, projected2.T, multiplier2.T


def solution(mesh):
    return jax.shard_map(
        per_device,
        mesh=mesh,
        in_specs=(P("row", "col"),) + (P("col", "row"),) * 4,
        out_specs=(P("col", "row"),) * 3,
        check_vma=False,
    )
```

time: 364 us -> 119 us (0.33)
  waiting for transfers between devices: 140 us -> 0 us
  blocking collectives: 125 us -> 0 us
  Pallas kernels: 0 us -> 116 us
  local copies, waits for them, and re-layouts: 29.9 us -> 0.01 us
  other arithmetic: 28.2 us -> 2 us
  matrix products: 25.8 us -> 0 us
  between operations: 14.1 us -> 0.69 us
    all_gather x2 -> x0, waiting for transfers between devices: 140 us -> none  [per_device(): gathered = lax.all_gather(change, 'row', axis=1, tiled=True)]
    all_to_all x6 -> x0, blocking collectives: 125 us -> none  [the longest x2 62.8 us: sum_at_owner(): lax.all_to_all(tiles, axis, split_axis=0, concat_axis=0, tiled=True)]
    pallas_call x0 -> x1, Pallas kernels: none -> 116 us  [run_kernel(): pl.pallas_call(kernel, out_shape=[jax.ShapeDtypeStruct((U, 8, KC), F32)]...]
    dot_general x2 -> x0, matrix products: 25.8 us -> none  [per_device(): jnp.dot(hessian, gathered, precision=lax.Precision.HIGHEST, preferred_ele...]
    unnamed x15 -> x6, local copies, waits for them, and re-layouts: 19.6 us -> 0.01 us
    all_to_all x4 -> x0, other arithmetic: 11.3 us -> none  [the longest x2 5.63 us: per_device(): lax.all_to_all(shaped, 'row', split_axis=3, concat_axis=0, tiled=True)]
    unnamed x2 -> x0, other arithmetic: 7.59 us -> none
    sub x3 -> x0, other arithmetic: 6.13 us -> none  [the longest x2 4.03 us: per_device(): change = iterate - dense_weight]
  transfers between devices with their start and end apart: 2 -> 0, of which waited for: 2 -> 0; matrix products, arithmetic and copies ran while one was open for 0% -> 0% of each run, Pallas kernels for 0% -> 0%
where the time goes in v2:
time: 119 us
  Pallas kernels  116 us (97%)
  other arithmetic  2 us (2%)
    pallas_call x1, Pallas kernels, run_kernel(): pl.pallas_call(kernel, out_shape=[jax.ShapeDtypeStruct((U, 8, KC), F32)]...  116 us

profile of v2, /device:TPU:8, one launch (start us, length us, event | category | flops | bytes accessed | tf_op | source)
XLA Modules:
  0.0 118.7 jit_solution(1178605330822762480)
XLA Ops:
  0.6 0.0 copy-start
  0.6 0.0 copy-start.1
  0.7 0.0 copy-start.2
  0.7 115.9 %shard_map.76 = (f32[4,8,1792]{2,1,0:T(8,128)}, f32[4,8,1792]{2,1,0:T(8,128)}) custom-call(f32[448,1792]{1,0:T(8,128)} %h_ref.1, f32[4,8,1792]{2,1,0:T(8,128)} %bitcast.91, f32[4,8,1792]{2,1,0:T(8,128)} %bitcast.92, f32[4,8,1792]{2,1,0:T(8,128)} %bitcast.90, s32[4,8,1792]{2,1,0:T(8,128)} %bitcast.89), custom_call_target="tpu_custom_call" | custom-call | tf_op jit(solution)/shard_map/pallas_call | solution.py:458
  116.6 0.0 copy-done
  116.6 0.0 copy-done.1
  116.6 0.0 copy-done.2
  116.6 2.0 %subtract_bitcast_fusion = (f32[1792,32]{0,1:T(8,128)}, f32[1792,32]{0,1:T(8,128)}, f32[1792,32]{0,1:T(8,128)}) fusion(s32[1792,32]{0,1:T(8,128)S(1)} %copy-done, f32[1792,32]{0,1:T(8,128)S(1)} %copy-done.1, f32[4,8,1792]{2,1,0:T(8,128)} %get-tuple-element.6, f32[1792,32]{0,1:T(8,128)S(1)} %copy-done.2, f32[4,8,1792]{2,1,0:T(8,128)} %get-tuple-element.5), kind=kLoop, calls=%fused_computation.8 | loop fusion | flops 745472 | bytes 1835008 | tf_op jit(solution)/shard_map/transpose | solution.py:480
Async XLA Ops:
  0.6 116.0 %copy-start = (s32[1792,32]{0,1:T(8,128)S(1)}, s32[1792,32]{0,1:T(8,128)}, u32[]{:S(2)}) copy-start(s32[1792,32]{0,1:T(8,128)} %param.9) | copy-start | bytes 688132
  0.6 116.0 %copy-start.1 = (f32[1792,32]{0,1:T(8,128)S(1)}, f32[1792,32]{0,1:T(8,128)}, u32[]{:S(2)}) copy-start(f32[1792,32]{0,1:T(8,128)} %param.8) | copy-start | bytes 688132
  0.7 116.0 %copy-start.2 = (f32[1792,32]{0,1:T(8,128)S(1)}, f32[1792,32]{0,1:T(8,128)}, u32[]{:S(2)}) copy-start(f32[1792,32]{0,1:T(8,128)} %param.6) | copy-start | bytes 688132

commit v3 on v2

--- a/solution.py
+++ b/solution.py
@@ -1,3 +1,5 @@
+import math
+
 import jax
 import jax.numpy as jnp
 from jax import lax
@@ -17,28 +19,32 @@
 ORDER = (
     ("ag0", 1, 0), ("ag0", 2, 0), ("ag0", 3, 0), ("gx", 0, 0), ("rel", 0, 0), ("ga", 0, 1), ("gb", 0, 1),
     ("gx", 1, 0), ("rel", 1, 0), ("gb", 1, 1), ("ga", 1, 1), ("gx", 2, 0), ("rel", 2, 0), ("ga", 2, 1),
-    ("gb", 2, 1), ("gx", 3, 0), ("rel", 3, 0), ("gb", 3, 1), ("ga", 3, 1), ("gpb", 0, 1), ("gpa", 0, 1),
-    ("gb", 0, 2), ("ga", 0, 2), ("gpa", 1, 1), ("gpb", 1, 1), ("ga", 1, 2), ("gb", 1, 2), ("gpb", 2, 1),
-    ("gpa", 2, 1), ("ga", 2, 2), ("gb", 2, 2), ("gpb", 3, 1), ("gpa", 3, 1), ("ga", 3, 2), ("gb", 3, 2),
-    ("gpa", 0, 2), ("gpb", 0, 2), ("ga", 0, 3), ("gb", 0, 3), ("gpb", 1, 2), ("gpa", 1, 2), ("ga", 1, 3),
-    ("gb", 1, 3), ("gpb", 2, 2), ("gpa", 2, 2), ("gb", 2, 3), ("ga", 2, 3), ("gpb", 3, 2), ("gpa", 3, 2),
+    ("gb", 2, 1), ("gx", 3, 0), ("rel", 3, 0), ("ga", 3, 1), ("gb", 3, 1), ("gpa", 0, 1), ("gpb", 0, 1),
+    ("gb", 0, 2), ("ga", 0, 2), ("gpb", 1, 1), ("gpa", 1, 1), ("gb", 1, 2), ("ga", 1, 2), ("gpa", 2, 1),
+    ("gpb", 2, 1), ("ga", 2, 2), ("gb", 2, 2), ("gpb", 3, 1), ("gpa", 3, 1), ("ga", 3, 2), ("gb", 3, 2),
+    ("gpb", 0, 2), ("gpa", 0, 2), ("ga", 0, 3), ("gb", 0, 3), ("gpa", 1, 2), ("gpb", 1, 2), ("gb", 1, 3),
+    ("ga", 1, 3), ("gpb", 2, 2), ("gpa", 2, 2), ("gb", 2, 3), ("ga", 2, 3), ("gpb", 3, 2), ("gpa", 3, 2),
     ("ga", 3, 3), ("gb", 3, 3), ("rel2", 0, 0), ("rel2", 1, 0), ("gpb", 0, 3), ("rel2", 2, 0), ("rel2", 3, 0),
     ("gpb", 1, 3), ("ga", 0, 4), ("gpb", 2, 3), ("gpb", 3, 3), ("ga", 1, 4), ("mm", 0, 0), ("ga", 2, 4),
-    ("ga", 3, 4), ("mm", 0, 1), ("mm", 1, 0), ("mm", 1, 1), ("mm", 2, 0), ("ry", 0, 0), ("ry", 0, 1),
-    ("mm", 2, 1), ("mm", 3, 0), ("ry", 1, 1), ("ry", 1, 0), ("xhi", 0, 0), ("mm", 3, 1), ("ry", 2, 1),
-    ("ry", 2, 0), ("xhi", 1, 0), ("ay1", 0, 0), ("ry", 3, 1), ("ry", 3, 0), ("xhi", 2, 0), ("ay2", 0, 0),
-    ("ay2", 0, 1), ("ay1", 1, 0), ("xhi", 3, 0), ("crel", 0, 0), ("ay1", 2, 0), ("mmt", 0, 0), ("ay2", 1, 1),
-    ("ay2", 1, 0), ("crel", 1, 0), ("ay1", 3, 0), ("ay2", 2, 0), ("ay2", 2, 1), ("mmt", 0, 1), ("ra", 0, 1),
-    ("rb", 0, 1), ("crel", 2, 0), ("mmt", 1, 0), ("rpa", 0, 1), ("rpb", 0, 1), ("ra", 0, 2), ("rb", 0, 2),
-    ("ay2", 3, 0), ("ay2", 3, 1), ("crel", 3, 0), ("mmt", 1, 1), ("ra", 1, 1), ("mmt", 2, 0), ("rpa", 0, 2),
-    ("rpb", 0, 2), ("ra", 0, 3), ("rb", 0, 3), ("rb", 1, 1), ("rpa", 1, 1), ("rpb", 1, 1), ("mmt", 2, 1),
-    ("ra", 1, 2), ("mmt", 3, 0), ("rpb", 0, 3), ("ra", 0, 4), ("ra", 2, 1), ("rpa", 1, 2), ("rb", 2, 1),
-    ("rpa", 2, 1), ("rb", 1, 2), ("mmt", 3, 1), ("rpb", 1, 2), ("rpf", 0, 0), ("ra", 1, 3), ("rpb", 2, 1),
-    ("ra", 3, 1), ("rb", 3, 1), ("rb", 2, 2), ("ra", 2, 2), ("rb", 1, 3), ("rpa", 2, 2), ("rpb", 3, 1),
-    ("rpb", 1, 3), ("rpa", 3, 1), ("rpb", 2, 2), ("fin", 0, 0), ("ra", 1, 4), ("rb", 3, 2), ("ra", 3, 2),
-    ("rb", 2, 3), ("ra", 2, 3), ("rpa", 3, 2), ("rpb", 3, 2), ("rpf", 1, 0), ("rpb", 2, 3), ("ra", 3, 3),
-    ("rb", 3, 3), ("fin", 1, 0), ("ra", 2, 4), ("rpb", 3, 3), ("rpf", 2, 0), ("ra", 3, 4), ("fin", 2, 0),
-    ("rpf", 3, 0), ("fin", 3, 0),
+    ("ga", 3, 4), ("mm", 0, 1), ("mm", 1, 0), ("mm", 1, 1), ("ry", 0, 0), ("ry", 0, 2), ("ry", 0, 1),
+    ("ry", 0, 3), ("mm", 2, 0), ("ry", 1, 0), ("ry", 1, 2), ("mm", 2, 1), ("xhi", 0, 0), ("ry", 1, 3),
+    ("xhi", 0, 1), ("ry", 1, 1), ("mm", 3, 0), ("xhi", 1, 0), ("ry", 2, 2), ("ry", 2, 0), ("mm", 3, 1),
+    ("xhi", 1, 1), ("ay1", 0, 0), ("ry", 2, 1), ("ry", 2, 3), ("ay1", 0, 1), ("crel0", 0, 0), ("ry", 3, 0),
+    ("ry", 3, 2), ("xhi", 2, 0), ("ay1", 1, 0), ("ry", 3, 1), ("ry", 3, 3), ("ay2", 0, 0), ("ay2", 0, 2),
+    ("ay1", 1, 1), ("xhi", 2, 1), ("crel0", 1, 0), ("ay2", 0, 1), ("ay2", 0, 3), ("xhi", 3, 0), ("ay2", 1, 0),
+    ("ay2", 1, 2), ("ay1", 2, 0), ("xhi", 3, 1), ("crel", 0, 0), ("ay2", 1, 1), ("ay2", 1, 3), ("ay1", 2, 1),
+    ("crel0", 2, 0), ("mmt", 0, 0), ("ay2", 2, 0), ("ay2", 2, 2), ("ay1", 3, 0), ("ay1", 3, 1),
+    ("crel", 1, 0), ("crel0", 3, 0), ("mmt", 0, 1), ("ra", 0, 1), ("ay2", 2, 1), ("ay2", 2, 3), ("mmt", 1, 0),
+    ("rb", 0, 1), ("ay2", 3, 2), ("ay2", 3, 0), ("crel", 2, 0), ("ay2", 3, 3), ("rpa", 0, 1), ("rpb", 0, 1),
+    ("ay2", 3, 1), ("mmt", 1, 1), ("ra", 0, 2), ("ra", 1, 1), ("crel", 3, 0), ("mmt", 2, 0), ("rb", 0, 2),
+    ("rpa", 0, 2), ("rpb", 0, 2), ("rb", 1, 1), ("rpb", 1, 1), ("rpa", 1, 1), ("mmt", 2, 1), ("ra", 0, 3),
+    ("mmt", 3, 0), ("rb", 0, 3), ("rpb", 0, 3), ("ra", 1, 2), ("rpa", 1, 2), ("ra", 2, 1), ("rb", 2, 1),
+    ("rpa", 2, 1), ("rb", 1, 2), ("mmt", 3, 1), ("ra", 0, 4), ("rpb", 1, 2), ("rpb", 2, 1), ("ra", 3, 1),
+    ("rb", 3, 1), ("ra", 1, 3), ("rpf", 0, 0), ("rb", 2, 2), ("ra", 2, 2), ("rb", 1, 3), ("rpa", 2, 2),
+    ("rpa", 3, 1), ("rpb", 3, 1), ("rpb", 1, 3), ("fin", 0, 0), ("rpb", 2, 2), ("ra", 3, 2), ("rb", 3, 2),
+    ("ra", 1, 4), ("rb", 2, 3), ("ra", 2, 3), ("rpb", 3, 2), ("rpa", 3, 2), ("rpf", 1, 0), ("rpb", 2, 3),
+    ("ra", 3, 3), ("rb", 3, 3), ("fin", 1, 0), ("ra", 2, 4), ("rpb", 3, 3), ("rpf", 2, 0), ("ra", 3, 4),
+    ("rpf", 3, 0), ("fin", 2, 0), ("fin", 3, 0),
 )
 
 
@@ -46,7 +52,7 @@
     h_ref, w_ref, i_ref, m_ref, k_ref, c1_out, g1_out,
     wv, iv, mv, kv, c0_ref, a_ref,
     hbuf, hhi, hlo, xs_ref, xall, pbuf, rb1, rb2, vbuf, xb, c1all, cs_ref, qbuf,
-    rx1, rza, rzb, rpa, rpb, rxf, ab, ch, ai, ci, ss, rs, hs,
+    rx1, rza, rzb, rpa, rpb, rxf, ab, ch, ai, ci, tally, ss, rs, hs, bulk,
 ):
     row = lax.axis_index("row")
     col = lax.axis_index("col")
@@ -88,9 +94,8 @@
     y_if0 = 2 * ya_b1 + ya_b0
     y_if1 = 2 * e1 + (1 - e0)
     yd = (1 - x) * y_if0 + x * y_if1
-    md = 2 * ((q0[1] // 2) * xh + (q0[0] // 2) * (1 - xh) + z // 4 - 2 * (((q0[1] // 2) * xh + (q0[0] // 2) * (1 - xh)) * (z // 4)))
-    t0 = (q0[1] % 2) * xh + (q0[0] % 2) * (1 - xh)
-    md = md + t0 + (z // 2) % 2 - 2 * (t0 * ((z // 2) % 2))
+    qx = (1 - xh) * q0[0] + xh * q0[1]
+    md = 2 * ((qx // 2 + z // 4) % 2) + (qx + z // 2) % 2
     dev_mid = ((y // 2) * 16 + z * 2 + k, yd * 2 + x)
     dev_home = (xh * 16 + z * 2 + k, 4 * x + md)
     dev_zz = [(x * 16 + (2 * md + h) * 2 + k, col) for h in range(2)]
@@ -132,7 +137,7 @@
         xall[u, x, z] = c0_ref[u]
 
     names = {}
-    sends = []
+    sent = {}
     moves = []
 
     def sem(name):
@@ -140,12 +145,12 @@
 
     def send(name, src, dst, dev):
         i = sem(name)
-        c = pltpu.make_async_remote_copy(
-            src_ref=src, dst_ref=dst, send_sem=ss.at[i], recv_sem=rs.at[i],
+        u = int(name.split(".")[0][-1]) if name != "h" else U
+        sent[u] = sent.get(u, 0) + math.prod(src.shape)
+        pltpu.make_async_remote_copy(
+            src_ref=src, dst_ref=dst, send_sem=bulk.at[u], recv_sem=rs.at[i],
             device_id=dev, device_id_type=MESH,
-        )
-        c.start()
-        sends.append(c)
+        ).start()
 
     def move(name, recv, src, dst, dev):
         i = sem(name)
@@ -174,6 +179,7 @@
 
     LO = pl.ds(0, KR)
     HI = pl.ds(KR, KR)
+    COLS = (pl.ds(0, 512), pl.ds(512, 384))
 
     def split_rows(part):
         @pl.loop(0, 28)
@@ -254,12 +260,12 @@
             @pl.loop(0, 2)
             def _(j):
                 mm_part(u, pl.multiple_of(j * 256, 256), 256)
-
-            return
-        mm_part(u, 512, 256)
-        mm_part(u, 768, 128)
-        send(f"r1{u}.0", pbuf.at[u, 0, pl.ds(4 * (1 - f1[0]), 4)], rb1.at[u, 0], dev_y1)
-        send(f"r1{u}.1", pbuf.at[u, 1, pl.ds(4 * (1 - f1[1]), 4)], rb1.at[u, 1], dev_y3)
+        else:
+            mm_part(u, 512, 256)
+            mm_part(u, 768, 128)
+        for hf, dev in ((0, dev_y1), (1, dev_y3)):
+            src = pbuf.at[u, hf, pl.ds(4 * (1 - f1[hf]), 4), :, COLS[s]]
+            send(f"r1{u}.{hf}{s}", src, rb1.at[u, hf, :, :, COLS[s]], dev)
 
     def split_half(src, u, half, dst, width):
         @pl.loop(0, 4)
@@ -270,31 +276,38 @@
             dst[pl.ds(pl.multiple_of(r0, 16), 16), :] = hi
             dst[pl.ds(pl.multiple_of(128 + r0, 16), 16), :] = (v - hi.astype(F32)).astype(BF16)
 
-    def ry(u, hf):
+    def ry(u, s):
+        hf, cc = s // 2, COLS[s % 2]
         dev2 = (dev_y3, dev_y1)[hf]
-        wait(f"r1{u}.{hf}", rb1.at[u, hf])
+        wait(f"r1{u}.{hf}{s % 2}", rb1.at[u, hf, :, :, cc])
         base = 4 * f1[hf]
         o = 2 * (1 - f2[hf])
-        pbuf[u, hf, pl.ds(base + o, 2)] = pbuf[u, hf, pl.ds(base + o, 2)] + rb1[u, hf, pl.ds(o, 2)]
-        send(f"r2{u}.{hf}", pbuf.at[u, hf, pl.ds(base + o, 2)], rb2.at[u, hf], dev2)
+        pair = pl.ds(base + o, 2)
+        pbuf[u, hf, pair, :, cc] = pbuf[u, hf, pair, :, cc] + rb1[u, hf, pl.ds(o, 2), :, cc]
+        send(f"r2{u}.{hf}{s % 2}", pbuf.at[u, hf, pair, :, cc], rb2.at[u, hf, :, :, cc], dev2)
         o = 2 * f2[hf]
-        vbuf[u, hf] = pbuf[u, hf, pl.ds(base + o, 2)] + rb1[u, hf, pl.ds(o, 2)]
+        vbuf[u, hf, :, :, cc] = pbuf[u, hf, pl.ds(base + o, 2), :, cc] + rb1[u, hf, pl.ds(o, 2), :, cc]
 
     def xhi(u, s):
-        for i in range(2):
-            wait(f"a{u}.{i}", ab.at[u, i])
-        vbuf[u, xh] = vbuf[u, xh] + ab[u]
+        cc = COLS[s]
+        if s == 0:
+            for i in range(2):
+                wait(f"a{u}.{i}", ab.at[u, i])
+        vbuf[u, xh, :, :, cc] = vbuf[u, xh, :, :, cc] + ab[u, :, :, cc]
         for hf in range(2):
-            wait(f"r2{u}.{hf}", rb2.at[u, hf])
-            vbuf[u, hf] = vbuf[u, hf] + rb2[u, hf]
-        send(f"xh{u}", vbuf.at[u], xb.at[u], dev_xh)
+            wait(f"r2{u}.{hf}{s}", rb2.at[u, hf, :, :, cc])
+            vbuf[u, hf, :, :, cc] = vbuf[u, hf, :, :, cc] + rb2[u, hf, :, :, cc]
+        send(f"xh{u}.{s}", vbuf.at[u, :, :, :, cc], xb.at[u, :, :, :, cc], dev_xh)
 
     def ay1(u, s):
-        wait(f"xh{u}", xb.at[u])
+        cc = COLS[s]
+        wait(f"xh{u}.{s}", xb.at[u, :, :, :, cc])
         for hf, dev in ((0, dev_y3), (1, dev_y1)):
-            slot = c1all.at[u, hf, pl.ds(2 * q[hf], 2)]
-            c1all[u, hf, pl.ds(2 * q[hf], 2)] = vbuf[u, hf] + xb[u, hf]
-            send(f"g1{u}.{hf}", slot, slot, dev)
+            slot = c1all.at[u, hf, pl.ds(2 * q[hf], 2), :, cc]
+            c1all[u, hf, pl.ds(2 * q[hf], 2), :, cc] = vbuf[u, hf, :, :, cc] + xb[u, hf, :, :, cc]
+            send(f"g1{u}.{hf}{s}", slot, slot, dev)
+
+    def crel0(u, s):
         for i in range(2):
             move(f"cs{u}.{i}", sem(f"c{u}.0") + hpart, c1all.at[u, xh, 2 * md + i], ci.at[u, hpart], dev_zz[i])
 
@@ -312,12 +325,13 @@
             wait(f"c{u}.{h}", ci.at[u, h])
         move(f"ct{u}", sem(f"ch{u}"), ci.at[u], ch.at[u], dev_home)
 
-    def ay2(u, hf):
+    def ay2(u, s):
+        hf, cc = s // 2, COLS[s % 2]
         dev2 = (dev_y1, dev_y3)[hf]
         o = 4 * f1[hf] + 2 * (1 - f2[hf])
-        wait(f"g1{u}.{hf}", c1all.at[u, hf, pl.ds(o, 2)])
-        slot = c1all.at[u, hf, pl.ds(4 * f1[hf], 4)]
-        send(f"g2{u}.{hf}", slot, slot, dev2)
+        wait(f"g1{u}.{hf}{s % 2}", c1all.at[u, hf, pl.ds(o, 2), :, cc])
+        slot = c1all.at[u, hf, pl.ds(4 * f1[hf], 4), :, cc]
+        send(f"g2{u}.{hf}{s % 2}", slot, slot, dev2)
 
     def mmt_part(u, c0, n):
         r = lax.dot_general(cs_ref[...], hhi[:, pl.ds(c0, n)], NN, preferred_element_type=F32)
@@ -327,7 +341,8 @@
     def mmt(u, s):
         if s == 0:
             for hf in range(2):
-                wait(f"g2{u}.{hf}", c1all.at[u, hf, pl.ds(4 * (1 - f1[hf]), 4)])
+                for c in range(2):
+                    wait(f"g2{u}.{hf}{c}", c1all.at[u, hf, pl.ds(4 * (1 - f1[hf]), 4), :, COLS[c]])
             for half in range(2):
                 split_half(c1all, u, half, cs_ref, KR)
 
@@ -411,7 +426,7 @@
 
     stages = dict(
         ag0=ag0, ga=ga, gb=gb, gx=gx, gpa=gpa, gpb=gpb, mm=mm, ry=ry, xhi=xhi, ay1=ay1, ay2=ay2,
-        mmt=mmt, ra=ra, rb=rb, rpa=rpa_, rpb=rpb_, rpf=rpf, fin=fin, rel=rel, rel2=rel2, crel=crel,
+        mmt=mmt, ra=ra, rb=rb, rpa=rpa_, rpb=rpb_, rpf=rpf, fin=fin, rel=rel, rel2=rel2, crel0=crel0, crel=crel,
     )
     pl.semaphore_wait(barrier, expected)
     ag0(0, 0)
@@ -420,8 +435,10 @@
     split_rows(k)
     for name, u, s in ORDER:
         stages[name](u, s)
-    for c in sends:
-        c.wait_send()
+    for u in range(U):
+        assert sent[u] == math.prod(tally.shape), sent
+        pltpu.make_async_copy(tally, tally, bulk.at[u]).wait()
+    pltpu.make_async_copy(h_ref, hbuf.at[k], bulk.at[U]).wait()
     for c, same in moves:
 
         @pl.when(jnp.logical_not(same))
@@ -452,8 +469,9 @@
         v((U, 8, KR), F32),
         v((U, 2, 8, KR), F32), v((U, 2, 8, KR), F32),
         v((U, 8, KC), F32), v((U, 2, 8, KR), F32),
+        v((44, 8, KC), F32),
         pltpu.SemaphoreType.DMA((NSEM,)), pltpu.SemaphoreType.DMA((NSEM,)),
-        pltpu.SemaphoreType.DMA((5,)),
+        pltpu.SemaphoreType.DMA((5,)), pltpu.SemaphoreType.DMA((U + 1,)),
     ]
     return pl.pallas_call(
         kernel,

time: 119 us -> 115 us (0.966)
  Pallas kernels: 116 us -> 111 us
    pallas_call x1, Pallas kernels: 116 us -> 111 us  [run_kernel(): pl.pallas_call(kernel, out_shape=[jax.ShapeDtypeStruct((U, 8, KC), F32)]...]
where the time goes in v3:
time: 115 us; the launch traced here: 114 us
  Pallas kernels  111 us (97%)
  other arithmetic  2 us (2%)
    pallas_call x1, Pallas kernels, run_kernel(): pl.pallas_call(kernel, out_shape=[jax.ShapeDtypeStruct((U, 8, KC), F32)]...  111 us

profile of v3, /device:TPU:8, one launch (start us, length us, event | category | flops | bytes accessed | tf_op | source)
XLA Modules:
  0.0 114.0 jit_solution(5319450855434106524)
XLA Ops:
  0.6 0.0 copy-start
  0.6 0.0 copy-start.1
  0.7 0.0 copy-start.2
  0.7 111.3 %shard_map.76 = (f32[4,8,1792]{2,1,0:T(8,128)}, f32[4,8,1792]{2,1,0:T(8,128)}) custom-call(f32[448,1792]{1,0:T(8,128)} %h_ref.1, f32[4,8,1792]{2,1,0:T(8,128)} %bitcast.91, f32[4,8,1792]{2,1,0:T(8,128)} %bitcast.92, f32[4,8,1792]{2,1,0:T(8,128)} %bitcast.90, s32[4,8,1792]{2,1,0:T(8,128)} %bitcast.89), custom_call_target="tpu_custom_call" | custom-call | tf_op jit(solution)/shard_map/pallas_call | solution.py:476
  111.9 0.0 copy-done
  111.9 0.0 copy-done.1
  111.9 0.0 copy-done.2
  112.0 2.0 %subtract_bitcast_fusion = (f32[1792,32]{0,1:T(8,128)}, f32[1792,32]{0,1:T(8,128)}, f32[1792,32]{0,1:T(8,128)}) fusion(s32[1792,32]{0,1:T(8,128)S(1)} %copy-done, f32[1792,32]{0,1:T(8,128)S(1)} %copy-done.1, f32[4,8,1792]{2,1,0:T(8,128)} %get-tuple-element.6, f32[1792,32]{0,1:T(8,128)S(1)} %copy-done.2, f32[4,8,1792]{2,1,0:T(8,128)} %get-tuple-element.5), kind=kLoop, calls=%fused_computation.8 | loop fusion | flops 745472 | bytes 1835008 | tf_op jit(solution)/shard_map/transpose | solution.py:498
Async XLA Ops:
  0.6 111.3 %copy-start = (s32[1792,32]{0,1:T(8,128)S(1)}, s32[1792,32]{0,1:T(8,128)}, u32[]{:S(2)}) copy-start(s32[1792,32]{0,1:T(8,128)} %param.9) | copy-start | bytes 688132
  0.6 111.3 %copy-start.1 = (f32[1792,32]{0,1:T(8,128)S(1)}, f32[1792,32]{0,1:T(8,128)}, u32[]{:S(2)}) copy-start(f32[1792,32]{0,1:T(8,128)} %param.8) | copy-start | bytes 688132
  0.7 111.3 %copy-start.2 = (f32[1792,32]{0,1:T(8,128)S(1)}, f32[1792,32]{0,1:T(8,128)}, u32[]{:S(2)}) copy-start(f32[1792,32]{0,1:T(8,128)} %param.6) | copy-start | bytes 688132

commit v4 on v3

--- a/solution.py
+++ b/solution.py
@@ -17,34 +17,34 @@
 
 
 ORDER = (
-    ("ag0", 1, 0), ("ag0", 2, 0), ("ag0", 3, 0), ("gx", 0, 0), ("rel", 0, 0), ("ga", 0, 1), ("gb", 0, 1),
-    ("gx", 1, 0), ("rel", 1, 0), ("gb", 1, 1), ("ga", 1, 1), ("gx", 2, 0), ("rel", 2, 0), ("ga", 2, 1),
-    ("gb", 2, 1), ("gx", 3, 0), ("rel", 3, 0), ("ga", 3, 1), ("gb", 3, 1), ("gpa", 0, 1), ("gpb", 0, 1),
-    ("gb", 0, 2), ("ga", 0, 2), ("gpb", 1, 1), ("gpa", 1, 1), ("gb", 1, 2), ("ga", 1, 2), ("gpa", 2, 1),
-    ("gpb", 2, 1), ("ga", 2, 2), ("gb", 2, 2), ("gpb", 3, 1), ("gpa", 3, 1), ("ga", 3, 2), ("gb", 3, 2),
-    ("gpb", 0, 2), ("gpa", 0, 2), ("ga", 0, 3), ("gb", 0, 3), ("gpa", 1, 2), ("gpb", 1, 2), ("gb", 1, 3),
-    ("ga", 1, 3), ("gpb", 2, 2), ("gpa", 2, 2), ("gb", 2, 3), ("ga", 2, 3), ("gpb", 3, 2), ("gpa", 3, 2),
-    ("ga", 3, 3), ("gb", 3, 3), ("rel2", 0, 0), ("rel2", 1, 0), ("gpb", 0, 3), ("rel2", 2, 0), ("rel2", 3, 0),
-    ("gpb", 1, 3), ("ga", 0, 4), ("gpb", 2, 3), ("gpb", 3, 3), ("ga", 1, 4), ("mm", 0, 0), ("ga", 2, 4),
-    ("ga", 3, 4), ("mm", 0, 1), ("mm", 1, 0), ("mm", 1, 1), ("ry", 0, 0), ("ry", 0, 2), ("ry", 0, 1),
-    ("ry", 0, 3), ("mm", 2, 0), ("ry", 1, 0), ("ry", 1, 2), ("mm", 2, 1), ("xhi", 0, 0), ("ry", 1, 3),
-    ("xhi", 0, 1), ("ry", 1, 1), ("mm", 3, 0), ("xhi", 1, 0), ("ry", 2, 2), ("ry", 2, 0), ("mm", 3, 1),
-    ("xhi", 1, 1), ("ay1", 0, 0), ("ry", 2, 1), ("ry", 2, 3), ("ay1", 0, 1), ("crel0", 0, 0), ("ry", 3, 0),
-    ("ry", 3, 2), ("xhi", 2, 0), ("ay1", 1, 0), ("ry", 3, 1), ("ry", 3, 3), ("ay2", 0, 0), ("ay2", 0, 2),
-    ("ay1", 1, 1), ("xhi", 2, 1), ("crel0", 1, 0), ("ay2", 0, 1), ("ay2", 0, 3), ("xhi", 3, 0), ("ay2", 1, 0),
-    ("ay2", 1, 2), ("ay1", 2, 0), ("xhi", 3, 1), ("crel", 0, 0), ("ay2", 1, 1), ("ay2", 1, 3), ("ay1", 2, 1),
-    ("crel0", 2, 0), ("mmt", 0, 0), ("ay2", 2, 0), ("ay2", 2, 2), ("ay1", 3, 0), ("ay1", 3, 1),
-    ("crel", 1, 0), ("crel0", 3, 0), ("mmt", 0, 1), ("ra", 0, 1), ("ay2", 2, 1), ("ay2", 2, 3), ("mmt", 1, 0),
-    ("rb", 0, 1), ("ay2", 3, 2), ("ay2", 3, 0), ("crel", 2, 0), ("ay2", 3, 3), ("rpa", 0, 1), ("rpb", 0, 1),
-    ("ay2", 3, 1), ("mmt", 1, 1), ("ra", 0, 2), ("ra", 1, 1), ("crel", 3, 0), ("mmt", 2, 0), ("rb", 0, 2),
-    ("rpa", 0, 2), ("rpb", 0, 2), ("rb", 1, 1), ("rpb", 1, 1), ("rpa", 1, 1), ("mmt", 2, 1), ("ra", 0, 3),
-    ("mmt", 3, 0), ("rb", 0, 3), ("rpb", 0, 3), ("ra", 1, 2), ("rpa", 1, 2), ("ra", 2, 1), ("rb", 2, 1),
-    ("rpa", 2, 1), ("rb", 1, 2), ("mmt", 3, 1), ("ra", 0, 4), ("rpb", 1, 2), ("rpb", 2, 1), ("ra", 3, 1),
-    ("rb", 3, 1), ("ra", 1, 3), ("rpf", 0, 0), ("rb", 2, 2), ("ra", 2, 2), ("rb", 1, 3), ("rpa", 2, 2),
-    ("rpa", 3, 1), ("rpb", 3, 1), ("rpb", 1, 3), ("fin", 0, 0), ("rpb", 2, 2), ("ra", 3, 2), ("rb", 3, 2),
-    ("ra", 1, 4), ("rb", 2, 3), ("ra", 2, 3), ("rpb", 3, 2), ("rpa", 3, 2), ("rpf", 1, 0), ("rpb", 2, 3),
-    ("ra", 3, 3), ("rb", 3, 3), ("fin", 1, 0), ("ra", 2, 4), ("rpb", 3, 3), ("rpf", 2, 0), ("ra", 3, 4),
-    ("rpf", 3, 0), ("fin", 2, 0), ("fin", 3, 0),
+    ("ag0", 1, 0), ("ag0", 2, 0), ("gx", 0, 0), ("rel", 0, 0), ("ga", 0, 1), ("gb", 0, 1), ("gx", 1, 0),
+    ("rel", 1, 0), ("ga", 1, 1), ("gb", 1, 1), ("gx", 2, 0), ("rel", 2, 0), ("ga", 2, 1), ("gb", 2, 1),
+    ("gpa", 0, 1), ("gpb", 0, 1), ("ga", 0, 2), ("gb", 0, 2), ("gpb", 1, 1), ("gpa", 1, 1), ("ga", 1, 2),
+    ("gb", 1, 2), ("gpb", 2, 1), ("gpa", 2, 1), ("ag0", 3, 0), ("ga", 2, 2), ("gb", 2, 2), ("gpb", 0, 2),
+    ("gpa", 0, 2), ("ga", 0, 3), ("gb", 0, 3), ("gx", 3, 0), ("gpb", 1, 2), ("gpa", 1, 2), ("rel", 3, 0),
+    ("ga", 1, 3), ("gb", 1, 3), ("gpa", 2, 2), ("gpb", 2, 2), ("ga", 3, 1), ("gb", 3, 1), ("hs", 0, 0),
+    ("ga", 2, 3), ("gb", 2, 3), ("gpb", 0, 3), ("gpb", 3, 1), ("ga", 0, 4), ("gpb", 1, 3), ("gpb", 2, 3),
+    ("gpa", 3, 1), ("gb", 3, 2), ("ga", 1, 4), ("mm", 0, 0), ("ga", 3, 2), ("gpb", 3, 2), ("rel2", 0, 0),
+    ("rel2", 3, 0), ("mm", 0, 1), ("ga", 2, 4), ("gb", 3, 3), ("gpa", 3, 2), ("mm", 1, 0), ("ry", 0, 0),
+    ("ry", 0, 2), ("ga", 3, 3), ("gpb", 3, 3), ("mm", 2, 0), ("ry", 0, 3), ("ry", 0, 1), ("mm", 1, 1),
+    ("ry", 1, 2), ("ry", 1, 0), ("rel2", 1, 0), ("ga", 3, 4), ("xhi", 0, 0), ("rel2", 2, 0), ("mm", 2, 1),
+    ("ry", 2, 0), ("ry", 2, 2), ("xhi", 0, 1), ("mm", 3, 0), ("ry", 1, 1), ("ry", 1, 3), ("mm", 3, 1),
+    ("ay1", 0, 0), ("ry", 2, 3), ("ry", 2, 1), ("xhi", 1, 0), ("ay1", 0, 1), ("crel0", 0, 0), ("xhi", 2, 0),
+    ("ry", 3, 0), ("ry", 3, 2), ("xhi", 1, 1), ("ry", 3, 1), ("ry", 3, 3), ("ay2", 0, 0), ("ay2", 0, 2),
+    ("xhi", 2, 1), ("ay1", 1, 0), ("ay2", 0, 1), ("ay2", 0, 3), ("xhi", 3, 0), ("ay1", 2, 0), ("xhi", 3, 1),
+    ("crel", 0, 0), ("ay1", 1, 1), ("crel0", 1, 0), ("ay2", 1, 0), ("ay2", 1, 2), ("ay1", 2, 1),
+    ("crel0", 2, 0), ("mmt", 0, 0), ("ay2", 1, 1), ("ay2", 1, 3), ("ay1", 3, 1), ("ay2", 2, 0), ("ay1", 3, 0),
+    ("ay2", 2, 2), ("mmt", 0, 1), ("ay2", 2, 1), ("ay2", 2, 3), ("crel0", 3, 0), ("ra", 0, 1), ("crel", 1, 0),
+    ("rb", 0, 1), ("mmt", 1, 0), ("rpa", 0, 1), ("rpb", 0, 1), ("ay2", 3, 3), ("ay2", 3, 1), ("ay2", 3, 0),
+    ("mmt", 1, 1), ("ra", 0, 2), ("rb", 0, 2), ("ay2", 3, 2), ("mmt", 2, 0), ("rpa", 0, 2), ("rpb", 0, 2),
+    ("ra", 1, 1), ("rb", 1, 1), ("mmt", 2, 1), ("rpb", 1, 1), ("rpa", 1, 1), ("rb", 0, 3), ("ra", 0, 3),
+    ("mmt", 3, 0), ("rpb", 0, 3), ("ra", 1, 2), ("rb", 1, 2), ("ra", 2, 1), ("rb", 2, 1), ("rpa", 2, 1),
+    ("rpb", 2, 1), ("mmt", 3, 1), ("rpa", 1, 2), ("ra", 0, 4), ("rpb", 1, 2), ("crel", 2, 0), ("crel", 3, 0),
+    ("rpf", 0, 0), ("ra", 3, 1), ("ra", 1, 3), ("rb", 3, 1), ("rb", 1, 3), ("ra", 2, 2), ("rb", 2, 2),
+    ("rpa", 2, 2), ("rpb", 2, 2), ("rpa", 3, 1), ("rpb", 3, 1), ("rpb", 1, 3), ("fin", 0, 0), ("rb", 3, 2),
+    ("ra", 3, 2), ("ra", 1, 4), ("rb", 2, 3), ("rpb", 2, 3), ("ra", 2, 3), ("rpb", 3, 2), ("rpf", 1, 0),
+    ("rpa", 3, 2), ("rb", 3, 3), ("ra", 3, 3), ("fin", 1, 0), ("rpf", 2, 0), ("rpb", 3, 3), ("ra", 2, 4),
+    ("ra", 3, 4), ("rpf", 3, 0), ("fin", 2, 0), ("fin", 3, 0),
 )
 
 
@@ -243,19 +243,16 @@
     NN = (((1,), (0,)), ((), ()))
 
     def mm_part(u, c0, n):
-        r = lax.dot_general(xs_ref[...], hhi[pl.ds(c0, n), :], NT, preferred_element_type=F32)
-        r2 = lax.dot_general(xs_ref[:128], hlo[pl.ds(c0, n), :], NT, preferred_element_type=F32)
+        r = lax.dot_general(xs_ref[u], hhi[pl.ds(c0, n), :], NT, preferred_element_type=F32)
+        r2 = lax.dot_general(xs_ref[u, :128], hlo[pl.ds(c0, n), :], NT, preferred_element_type=F32)
         v = (r[:128] + r[128:] + r2) * (-STEP)
         pbuf[u, :, :, :, pl.ds(c0, n)] = v.reshape(2, 8, 8, n)
 
     def mm(u, s):
         if s == 0:
             wait_gather(u)
-            if u == 0:
-                wait("h", hbuf.at[1 - k])
-                split_rows(1 - k)
             for half in range(2):
-                split_half(xall, u, half, xs_ref, KC)
+                split_half(xall, u, half, xs_ref.at[u], KC)
 
             @pl.loop(0, 2)
             def _(j):
@@ -266,6 +263,10 @@
         for hf, dev in ((0, dev_y1), (1, dev_y3)):
             src = pbuf.at[u, hf, pl.ds(4 * (1 - f1[hf]), 4), :, COLS[s]]
             send(f"r1{u}.{hf}{s}", src, rb1.at[u, hf, :, :, COLS[s]], dev)
+
+    def hs_(u, s):
+        wait("h", hbuf.at[1 - k])
+        split_rows(1 - k)
 
     def split_half(src, u, half, dst, width):
         @pl.loop(0, 4)
@@ -334,8 +335,8 @@
         send(f"g2{u}.{hf}{s % 2}", slot, slot, dev2)
 
     def mmt_part(u, c0, n):
-        r = lax.dot_general(cs_ref[...], hhi[:, pl.ds(c0, n)], NN, preferred_element_type=F32)
-        r2 = lax.dot_general(cs_ref[:128], hlo[:, pl.ds(c0, n)], NN, preferred_element_type=F32)
+        r = lax.dot_general(cs_ref[u], hhi[:, pl.ds(c0, n)], NN, preferred_element_type=F32)
+        r2 = lax.dot_general(cs_ref[u, :128], hlo[:, pl.ds(c0, n)], NN, preferred_element_type=F32)
         qbuf[u, :, :, :, pl.ds(c0, n)] = (r[:128] + r[128:] + r2).reshape(2, 8, 8, n)
 
     def mmt(u, s):
@@ -344,7 +345,7 @@
                 for c in range(2):
                     wait(f"g2{u}.{hf}{c}", c1all.at[u, hf, pl.ds(4 * (1 - f1[hf]), 4), :, COLS[c]])
             for half in range(2):
-                split_half(c1all, u, half, cs_ref, KR)
+                split_half(c1all, u, half, cs_ref.at[u], KR)
 
             @pl.loop(0, 4)
             def _(j):
@@ -426,7 +427,7 @@
 
     stages = dict(
         ag0=ag0, ga=ga, gb=gb, gx=gx, gpa=gpa, gpb=gpb, mm=mm, ry=ry, xhi=xhi, ay1=ay1, ay2=ay2,
-        mmt=mmt, ra=ra, rb=rb, rpa=rpa_, rpb=rpb_, rpf=rpf, fin=fin, rel=rel, rel2=rel2, crel0=crel0, crel=crel,
+        mmt=mmt, ra=ra, rb=rb, rpa=rpa_, rpb=rpb_, rpf=rpf, fin=fin, hs=hs_, rel=rel, rel2=rel2, crel0=crel0, crel=crel,
     )
     pl.semaphore_wait(barrier, expected)
     ag0(0, 0)
@@ -456,12 +457,12 @@
     scratch = [
         v((U, 8, KC), F32), v((U, 8, KC), F32), v((U, 8, KC), F32), v((U, 8, KC), jnp.int32),
         v((U, 8, KC), F32), v((U, 8, KC), F32),
-        v((2, 448, KC), F32), v((KR, KC), BF16), v((KR, KC), BF16), v((256, KC), BF16),
+        v((2, 448, KC), F32), v((KR, KC), BF16), v((KR, KC), BF16), v((U, 256, KC), BF16),
         v((U, 2, 8, 8, KC), F32),
         v((U, 2, 8, 8, KR), F32),
         v((U, 2, 4, 8, KR), F32), v((U, 2, 2, 8, KR), F32),
         v((U, 2, 2, 8, KR), F32), v((U, 2, 2, 8, KR), F32),
-        v((U, 2, 8, 8, KR), F32), v((256, KR), BF16),
+        v((U, 2, 8, 8, KR), F32), v((U, 256, KR), BF16),
         v((U, 2, 8, 8, KC), F32),
         v((U, 8, 8, KR), F32),
         v((U, 4, 8, KC), F32), v((U, 3, 8, KC), F32),

time: 115 us -> 107 us (0.930)
  Pallas kernels: 111 us -> 103 us
    pallas_call x1, Pallas kernels: 111 us -> 103 us  [run_kernel(): pl.pallas_call(kernel, out_shape=[jax.ShapeDtypeStruct((U, 8, KC), F32)]...]
where the time goes in v4:
time: 107 us; the launch traced here: 106 us
  Pallas kernels  103 us (96%)
  other arithmetic  2 us (2%)
    pallas_call x1, Pallas kernels, run_kernel(): pl.pallas_call(kernel, out_shape=[jax.ShapeDtypeStruct((U, 8, KC), F32)]...  103 us

profile of v4, /device:TPU:8, one launch (start us, length us, event | category | flops | bytes accessed | tf_op | source)
XLA Modules:
  0.0 105.8 jit_solution(16286970598978068167)
XLA Ops:
  0.6 0.0 copy-start
  0.6 0.0 copy-start.1
  0.7 0.0 copy-start.2
  0.7 103.1 %shard_map.76 = (f32[4,8,1792]{2,1,0:T(8,128)}, f32[4,8,1792]{2,1,0:T(8,128)}) custom-call(f32[448,1792]{1,0:T(8,128)} %h_ref.1, f32[4,8,1792]{2,1,0:T(8,128)} %bitcast.91, f32[4,8,1792]{2,1,0:T(8,128)} %bitcast.92, f32[4,8,1792]{2,1,0:T(8,128)} %bitcast.90, s32[4,8,1792]{2,1,0:T(8,128)} %bitcast.89), custom_call_target="tpu_custom_call" | custom-call | tf_op jit(solution)/shard_map/pallas_call | solution.py:477
  103.8 0.0 copy-done
  103.8 0.0 copy-done.1
  103.8 0.0 copy-done.2
  103.8 2.0 %subtract_bitcast_fusion = (f32[1792,32]{0,1:T(8,128)}, f32[1792,32]{0,1:T(8,128)}, f32[1792,32]{0,1:T(8,128)}) fusion(s32[1792,32]{0,1:T(8,128)S(1)} %copy-done, f32[1792,32]{0,1:T(8,128)S(1)} %copy-done.1, f32[4,8,1792]{2,1,0:T(8,128)} %get-tuple-element.6, f32[1792,32]{0,1:T(8,128)S(1)} %copy-done.2, f32[4,8,1792]{2,1,0:T(8,128)} %get-tuple-element.5), kind=kLoop, calls=%fused_computation.8 | loop fusion | flops 745472 | bytes 1835008 | tf_op jit(solution)/shard_map/transpose | solution.py:499
Async XLA Ops:
  0.6 103.2 %copy-start = (s32[1792,32]{0,1:T(8,128)S(1)}, s32[1792,32]{0,1:T(8,128)}, u32[]{:S(2)}) copy-start(s32[1792,32]{0,1:T(8,128)} %param.9) | copy-start | bytes 688132
  0.6 103.2 %copy-start.1 = (f32[1792,32]{0,1:T(8,128)S(1)}, f32[1792,32]{0,1:T(8,128)}, u32[]{:S(2)}) copy-start(f32[1792,32]{0,1:T(8,128)} %param.8) | copy-start | bytes 688132
  0.7 103.2 %copy-start.2 = (f32[1792,32]{0,1:T(8,128)S(1)}, f32[1792,32]{0,1:T(8,128)}, u32[]{:S(2)}) copy-start(f32[1792,32]{0,1:T(8,128)} %param.6) | copy-start | bytes 688132

commit v5 on v4

--- a/solution.py
+++ b/solution.py
@@ -407,7 +407,18 @@
         rpb_(u, 4)
         send(f"xf{u}", qbuf.at[u, xo, z, :, HI], rxf.at[u], dev_x)
 
+    def drain():
+        for c, same in moves:
+
+            @pl.when(jnp.logical_not(same))
+            def _():
+                c.wait_send()
+
+        moves.clear()
+
     def fin(u, s):
+        if u == 2:
+            drain()
         take_x(u, 0)
         wait(f"zb{u}.3", rzb.at[u, 2])
         wait(f"za{u}.4", rza.at[u, 3])
@@ -440,12 +451,7 @@
         assert sent[u] == math.prod(tally.shape), sent
         pltpu.make_async_copy(tally, tally, bulk.at[u]).wait()
     pltpu.make_async_copy(h_ref, hbuf.at[k], bulk.at[U]).wait()
-    for c, same in moves:
-
-        @pl.when(jnp.logical_not(same))
-        def _():
-            c.wait_send()
-
+    drain()
     assert len(names) <= NSEM, len(names)
 
 

time: 107 us -> 107 us (level)
  no operation moved by 1% of the time
where the time goes in v5:
time: 107 us; the launch traced here: 106 us
  Pallas kernels  103 us (96%)
  other arithmetic  2 us (2%)
    pallas_call x1, Pallas kernels, run_kernel(): pl.pallas_call(kernel, out_shape=[jax.ShapeDtypeStruct((U, 8, KC), F32)]...  103 us

profile of v5, /device:TPU:8, one launch (start us, length us, event | category | flops | bytes accessed | tf_op | source)
XLA Modules:
  0.0 105.8 jit_solution(1156588381129620914)
XLA Ops:
  0.6 0.0 copy-start
  0.6 0.0 copy-start.1
  0.7 0.0 copy-start.2
  0.7 103.1 %shard_map.76 = (f32[4,8,1792]{2,1,0:T(8,128)}, f32[4,8,1792]{2,1,0:T(8,128)}) custom-call(f32[448,1792]{1,0:T(8,128)} %h_ref.1, f32[4,8,1792]{2,1,0:T(8,128)} %bitcast.91, f32[4,8,1792]{2,1,0:T(8,128)} %bitcast.92, f32[4,8,1792]{2,1,0:T(8,128)} %bitcast.90, s32[4,8,1792]{2,1,0:T(8,128)} %bitcast.89), custom_call_target="tpu_custom_call" | custom-call | tf_op jit(solution)/shard_map/pallas_call | solution.py:483
  103.8 0.0 copy-done
  103.8 0.0 copy-done.1
  103.8 0.0 copy-done.2
  103.8 2.0 %subtract_bitcast_fusion = (f32[1792,32]{0,1:T(8,128)}, f32[1792,32]{0,1:T(8,128)}, f32[1792,32]{0,1:T(8,128)}) fusion(s32[1792,32]{0,1:T(8,128)S(1)} %copy-done, f32[1792,32]{0,1:T(8,128)S(1)} %copy-done.1, f32[4,8,1792]{2,1,0:T(8,128)} %get-tuple-element.6, f32[1792,32]{0,1:T(8,128)S(1)} %copy-done.2, f32[4,8,1792]{2,1,0:T(8,128)} %get-tuple-element.5), kind=kLoop, calls=%fused_computation.8 | loop fusion | flops 745472 | bytes 1835008 | tf_op jit(solution)/shard_map/transpose | solution.py:505
Async XLA Ops:
  0.6 103.1 %copy-start = (s32[1792,32]{0,1:T(8,128)S(1)}, s32[1792,32]{0,1:T(8,128)}, u32[]{:S(2)}) copy-start(s32[1792,32]{0,1:T(8,128)} %param.9) | copy-start | bytes 688132
  0.6 103.1 %copy-start.1 = (f32[1792,32]{0,1:T(8,128)S(1)}, f32[1792,32]{0,1:T(8,128)}, u32[]{:S(2)}) copy-start(f32[1792,32]{0,1:T(8,128)} %param.8) | copy-start | bytes 688132
  0.7 103.1 %copy-start.2 = (f32[1792,32]{0,1:T(8,128)S(1)}, f32[1792,32]{0,1:T(8,128)}, u32[]{:S(2)}) copy-start(f32[1792,32]{0,1:T(8,128)} %param.6) | copy-start | bytes 688132
